TPU v7x, 32 devices: a whole 2x2x4 slice. The times are simulated.
32 devices in a mesh: wide: 8 (over z, y), narrow: 4 (over x, core).
Axes of the slice: x: 2, y: 2, z: 4, core: 2. Of those that a mesh axis runs over, the one named last changes fastest.
Arguments:
- layer_input: bfloat16 [16384, 768], P(('wide', 'narrow')), may hold values from -9 to 9
- layer_cotangent: bfloat16 [16384, 768], P(('wide', 'narrow')), may hold values from -13 to 13
- attend_weight: float32 [3, 768, 768], P(None, 'wide', 'narrow'), may hold values from -0.21875 to 0.21875
- attend_first: float32 [3, 768, 768], P(None, 'wide', 'narrow'), may hold values from -16 to 16
- attend_second: float32 [3, 768, 768], P(None, 'wide', 'narrow'), may hold values from 7.86432 to 31.1296
- output_weight: float32 [768, 768], P('narrow', 'wide'), may hold values from -1.75 to 1.75
- output_first: float32 [768, 768], P('narrow', 'wide'), may hold values from -6 to 6
- output_second: float32 [768, 768], P('narrow', 'wide'), may hold values from 0.147456 to 0.589824
- gated_weight: float32 [2, 768, 2048], P(None, 'wide', 'narrow'), may hold values from -0.21875 to 0.21875
- gated_first: float32 [2, 768, 2048], P(None, 'wide', 'narrow'), may hold values from -6 to 6
- gated_second: float32 [2, 768, 2048], P(None, 'wide', 'narrow'), may hold values from 4.194304 to 16.384
- down_weight: float32 [2048, 768], P('narrow', 'wide'), may hold values from -0.125 to 0.125
- down_first: float32 [2048, 768], P('narrow', 'wide'), may hold values from -16 to 16
- down_second: float32 [2048, 768], P('narrow', 'wide'), may hold values from 7.86432 to 31.1296
- norm_gains: float32 [2, 768], P(None, 'wide'), may hold values from 0.5 to 1.5
- gains_first: float32 [2, 768], P(None, 'wide'), may hold values from -48 to 48
- gains_second: float32 [2, 768], P(None, 'wide'), may hold values from 58.9824 to 235.9296
Outputs:
- layer_output: bfloat16 [16384, 768], P(('wide', 'narrow'))
- input_grad: float32 [16384, 768], P(('wide', 'narrow'))
- grad_norm: float32 [], replicated
- new_attend: float32 [3, 768, 768], P(None, 'wide', 'narrow')
- new_attend_first: float32 [3, 768, 768], P(None, 'wide', 'narrow')
- new_attend_second: float32 [3, 768, 768], P(None, 'wide', 'narrow')
- new_output: float32 [768, 768], P('narrow', 'wide')
- new_output_first: float32 [768, 768], P('narrow', 'wide')
- new_output_second: float32 [768, 768], P('narrow', 'wide')
- new_gated: float32 [2, 768, 2048], P(None, 'wide', 'narrow')
- new_gated_first: float32 [2, 768, 2048], P(None, 'wide', 'narrow')
- new_gated_second: float32 [2, 768, 2048], P(None, 'wide', 'narrow')
- new_down: float32 [2048, 768], P('narrow', 'wide')
- new_down_first: float32 [2048, 768], P('narrow', 'wide')
- new_down_second: float32 [2048, 768], P('narrow', 'wide')
- new_gains: float32 [2, 768], P(None, 'wide')
- new_gains_first: float32 [2, 768], P(None, 'wide')
- new_gains_second: float32 [2, 768], P(None, 'wide')
All inputs are finite; a program needn't handle non-finite values.
Results may differ from a plain program's by a relative error of at most 0.012.
The roundings to bfloat16 on the way count: a program that leaves them out, or rounds other values in their place, can miss the bound.
Values may be sent and summed in bfloat16 or wider, within the bound.
No kernel may reach another device: no remote copies, remote signals or barrier semaphores. Data moves between devices by JAX's collectives and lax.ppermute only.
A program may use at most 128 MiB of HBM per device.

v0:
```python
import functools
import math

import jax
import jax.numpy as jnp
from jax import lax
from jax.experimental import pallas as pl
from jax.experimental.pallas import tpu as pltpu
from jax.sharding import PartitionSpec as P

D = 768
HD = 64
FF = 2048
L = 1024
ADAM_STEP = 5

EPSILON = 1e-05
WEIGHT_DECAY = 0.1
AVERAGING = 0.5

LOW = jnp.bfloat16
FULL = jnp.float32
QB = 256
MASKED = -1e30


def swap(value, axis, bit):
    size = lax.axis_size(axis)
    return lax.ppermute(value, axis, [(i, i ^ bit) for i in range(size)])


def wide_bits():
    top = lax.axis_size("wide").bit_length() - 1
    return [1 << b for b in range(top - 1, -1, -1)]


def block_masks():
    masks = [0]
    for bit in wide_bits():
        masks = masks + [m ^ bit for m in masks]
    return masks


def after(value, *done):
    return lax.optimization_barrier((value, done))[0]


def widen(held, bits):
    for bit in bits:
        held = jnp.concatenate([held, swap(held, "wide", bit)], axis=0)
    return held


def add(kept, received):
    return kept.astype(FULL) + received.astype(FULL)


def narrow_down(held, bits):
    for bit in bits:
        half = held.shape[0] // 2
        held = add(held[:half], swap(held[half:].astype(LOW), "wide", bit))
    return held


def tree_sum(value, axis):
    bits = [1 << b for b in range(lax.axis_size(axis).bit_length() - 1)]
    for bit in bits:
        value = value + swap(value, axis, bit)
    return value


def turn(value, cosine, sine, sign):
    width = value.shape[1]
    lane = lax.broadcasted_iota(jnp.int32, value.shape, 1) % HD
    other = jnp.where(
        lane < HD // 2,
        pltpu.roll(value, width - HD // 2, 1),
        pltpu.roll(value, HD // 2, 1),
    )
    reps = width // 128
    return value * jnp.concatenate([cosine] * reps, axis=1) + sign * other * jnp.concatenate(
        [sine] * reps, axis=1
    )


def nn(a, b):
    return lax.dot_general(a, b, (((1,), (0,)), ((), ())), preferred_element_type=FULL)


def nt(a, b):
    return lax.dot_general(a, b, (((1,), (1,)), ((), ())), preferred_element_type=FULL)


def diagonal(scores):
    key = lax.broadcasted_iota(jnp.int32, scores.shape, 0)
    query = lax.broadcasted_iota(jnp.int32, scores.shape, 1)
    return jnp.where(key <= query, scores, MASKED)


def flip(value):
    return value.astype(FULL).T


def attend_kernel(
    rows_ref, qka_ref, qkb_ref, voa_ref, vob_ref, cos_ref, sin_ref,
    q_ref, k_ref, v_ref, ctx_ref, lse_ref, hold,
):
    heads = q_ref.shape[0]
    width = heads * HD
    half = qka_ref.shape[0]

    def project(i, carry):
        rows = pl.ds(pl.multiple_of(i * QB, QB), QB)
        first, second = rows_ref[rows, :half], rows_ref[rows, half:]
        pair = nn(first, qka_ref[...]) + nn(second, qkb_ref[...])
        pair = turn(pair, cos_ref[rows, :], sin_ref[rows, :], 1.0)
        value = nn(first, voa_ref[:, :width]) + nn(second, vob_ref[:, :width])
        for h in range(heads):
            q_ref[h, rows, :] = (pair[:, h * HD : (h + 1) * HD] * (HD**-0.5)).astype(LOW)
            k_ref[h, rows, :] = pair[:, width + h * HD : width + (h + 1) * HD].astype(LOW)
            v_ref[h, rows, :] = value[:, h * HD : (h + 1) * HD].astype(LOW)
        return carry

    lax.fori_loop(0, L // QB, project, 0)

    def head(h, carry):
        turned = flip(v_ref[h]).astype(LOW)
        for i in range(L // QB):
            lo, hi = i * QB, (i + 1) * QB
            query = q_ref[h, lo:hi, :]
            diag = diagonal(nt(k_ref[h, lo:hi, :], query))
            peak = jnp.max(diag, axis=0, keepdims=True)
            if i:
                body = nt(k_ref[h, :lo, :], query)
                peak = jnp.maximum(peak, jnp.max(body, axis=0, keepdims=True))
            weight = jnp.exp(diag - peak)
            total = jnp.sum(weight, axis=0, keepdims=True)
            out = nn(turned[:, lo:hi], weight.astype(LOW))
            if i:
                weight = jnp.exp(body - peak)
                total = total + jnp.sum(weight, axis=0, keepdims=True)
                out = out + nn(turned[:, :lo], weight.astype(LOW))
            lse_ref[h, :, lo:hi] = peak + jnp.log(total)
            hold[h, lo:hi, :] = (out / total).T.astype(LOW)
        return carry

    lax.fori_loop(0, heads, head, 0)
    for h in range(heads):
        ctx_ref[:, h * HD : (h + 1) * HD] = hold[h]


def whole(array):
    zero = (0,) * array.ndim
    return pl.BlockSpec(array.shape, lambda *_: zero)


def columns(piece):
    if not isinstance(piece, tuple):
        return piece, whole(piece)
    array, width, j = piece
    return array, pl.BlockSpec((array.shape[0], width), lambda *_: (0, j))


def width_of(piece):
    return piece[1] if isinstance(piece, tuple) else piece.shape[1]


def attend_forward(rows, qk, vo, cosine, sine):
    heads = width_of(qk[0]) // 2 // HD
    headed = jax.ShapeDtypeStruct((heads, L, HD), LOW)
    outs = (
        headed, headed, headed,
        jax.ShapeDtypeStruct((L, heads * HD), LOW),
        jax.ShapeDtypeStruct((heads, 1, L), FULL),
    )
    args, specs = zip(*[columns(p) for p in (rows, *qk, *vo, cosine, sine)])
    return pl.pallas_call(
        attend_kernel,
        grid=(1,),
        in_specs=list(specs),
        out_specs=[whole(o) for o in outs],
        out_shape=outs,
        scratch_shapes=[pltpu.VMEM((heads, L, HD), LOW)],
        compiler_params=pltpu.CompilerParams(vmem_limit_bytes=40 << 20),
        cost_estimate=pl.CostEstimate(
            flops=8 * 10**9, bytes_accessed=8 << 20, transcendentals=2 << 20
        ),
        name="attend_forward",
    )(*args)


def attend_back_kernel(
    q_ref, k_ref, v_ref, lse_ref, dctx_ref, cos_ref, sin_ref,
    dqk_ref, dv_ref, dctx, dqk, dk_sum, dv_sum,
):
    heads = q_ref.shape[0]
    width = heads * HD
    for h in range(heads):
        dctx[h] = dctx_ref[:, h * HD : (h + 1) * HD]

    def head(h, carry):
        turned = flip(k_ref[h]).astype(LOW)
        for i in range(L // QB):
            lo, hi = i * QB, (i + 1) * QB
            query, back = q_ref[h, lo:hi, :], dctx[h, lo:hi, :]
            lse = lse_ref[h, :, lo:hi]
            prob = jnp.exp(diagonal(nt(k_ref[h, lo:hi, :], query)) - lse)
            grad = nt(v_ref[h, lo:hi, :], back)
            inner = jnp.sum(prob * grad, axis=0, keepdims=True)
            if i:
                prob_body = jnp.exp(nt(k_ref[h, :lo, :], query) - lse)
                grad_body = nt(v_ref[h, :lo, :], back)
                inner = inner + jnp.sum(prob_body * grad_body, axis=0, keepdims=True)
            score = (prob * (grad - inner)).astype(LOW)
            dv_sum[h, lo:hi, :] = nn(prob.astype(LOW), back)
            dk_sum[h, lo:hi, :] = nn(score, query)
            dquery = nn(turned[:, lo:hi], score)
            if i:
                score = (prob_body * (grad_body - inner)).astype(LOW)
                dv_sum[h, :lo, :] += nn(prob_body.astype(LOW), back)
                dk_sum[h, :lo, :] += nn(score, query)
                dquery = dquery + nn(turned[:, :lo], score)
            dqk[h, lo:hi, :] = (dquery * (HD**-0.5)).T
        return carry

    lax.fori_loop(0, heads, head, 0)

    def finish(i, carry):
        rows = pl.ds(pl.multiple_of(i * QB, QB), QB)
        pair = jnp.concatenate(
            [dqk[h, rows, :] for h in range(heads)] + [dk_sum[h, rows, :] for h in range(heads)],
            axis=1,
        )
        dqk_ref[rows, :] = turn(pair, cos_ref[rows, :], sin_ref[rows, :], -1.0).astype(LOW)
        dv_ref[rows, :] = jnp.concatenate(
            [dv_sum[h, rows, :] for h in range(heads)], axis=1
        ).astype(LOW)
        return carry

    lax.fori_loop(0, L // QB, finish, 0)


def attend_backward(q, k, v, lse, dctx, cosine, sine):
    heads = q.shape[0]
    return pl.pallas_call(
        attend_back_kernel,
        out_shape=(
            jax.ShapeDtypeStruct((L, 2 * heads * HD), LOW),
            jax.ShapeDtypeStruct((L, heads * HD), LOW),
        ),
        scratch_shapes=[
            pltpu.VMEM((heads, L, HD), LOW),
            pltpu.VMEM((heads, L, HD), FULL),
            pltpu.VMEM((heads, L, HD), FULL),
            pltpu.VMEM((heads, L, HD), FULL),
        ],
        compiler_params=pltpu.CompilerParams(vmem_limit_bytes=40 << 20),
        cost_estimate=pl.CostEstimate(
            flops=9 * 10**9, bytes_accessed=8 << 20, transcendentals=2 << 20
        ),
        name="attend_backward",
    )(q, k, v, lse, dctx, cosine, sine)


def by_rows(kernel, name, flops, row_args, fixed, outs, sums=0):
    specs = [pl.BlockSpec((QB, r.shape[1]), lambda i: (i, 0)) for r in row_args]
    held, held_specs = zip(*[columns(p) for p in fixed])
    shapes = [jax.ShapeDtypeStruct((L, w), t) for w, t in outs]
    out_specs = [pl.BlockSpec((QB, w), lambda i: (i, 0)) for w, _ in outs]
    shapes += [jax.ShapeDtypeStruct((1, D), FULL)] * sums
    out_specs += [pl.BlockSpec((1, D), lambda i: (0, 0))] * sums
    return pl.pallas_call(
        kernel,
        grid=(L // QB,),
        in_specs=specs + list(held_specs),
        out_specs=out_specs,
        out_shape=shapes,
        compiler_params=pltpu.CompilerParams(vmem_limit_bytes=48 << 20),
        cost_estimate=pl.CostEstimate(
            flops=int(flops), bytes_accessed=16 << 20, transcendentals=1 << 20
        ),
        name=name,
    )(*row_args, *held)


def rms_scale(residual):
    return lax.rsqrt(jnp.mean(residual * residual, axis=1, keepdims=True) + EPSILON)


def norm_back(scaled, normed, inv):
    return inv * (scaled - normed * jnp.mean(scaled * normed, axis=1, keepdims=True))


def column_sum(sum_ref, value):
    @pl.when(pl.program_id(0) == 0)
    def _():
        sum_ref[...] = jnp.zeros_like(sum_ref)

    sum_ref[...] += jnp.sum(value, axis=0, keepdims=True)


def project_kernel(one_ref, two_ref, voa_ref, vob_ref, voc_ref, vod_ref, out_ref):
    width = one_ref.shape[1]
    half = voa_ref.shape[0]
    one, two = one_ref[...], two_ref[...]
    out_ref[:, :half] = (nt(one, voa_ref[:, width:]) + nt(two, voc_ref[:, width:])).astype(LOW)
    out_ref[:, half:] = (nt(one, vob_ref[:, width:]) + nt(two, vod_ref[:, width:])).astype(LOW)


def gate_up(hidden, ga_ref, gb_ref, ua_ref, ub_ref, gate_ref, up_ref, act_ref):
    half = ga_ref.shape[0]
    first, second = hidden[:, :half], hidden[:, half:]
    gate = nn(first, ga_ref[...]) + nn(second, gb_ref[...])
    up = nn(first, ua_ref[...]) + nn(second, ub_ref[...])
    gate_ref[...] = gate
    up_ref[...] = up
    act_ref[...] = (gate * jax.nn.sigmoid(gate) * up).astype(LOW)


def enter_kernel(
    rows_ref, mine_ref, theirs_ref, gain_ref, ga_ref, gb_ref, ua_ref, ub_ref,
    normed_ref, inv_ref, hidden_ref, gate_ref, up_ref, act_ref,
):
    residual = rows_ref[...].astype(FULL) + add(mine_ref[...], theirs_ref[...])
    inv = rms_scale(residual)
    normed = residual * inv
    hidden = (normed * gain_ref[...]).astype(LOW)
    normed_ref[...] = normed
    inv_ref[...] = inv
    hidden_ref[...] = hidden
    gate_up(hidden, ga_ref, gb_ref, ua_ref, ub_ref, gate_ref, up_ref, act_ref)


def more_kernel(hidden_ref, ga_ref, gb_ref, ua_ref, ub_ref, gate_ref, up_ref, act_ref):
    gate_up(hidden_ref[...], ga_ref, gb_ref, ua_ref, ub_ref, gate_ref, up_ref, act_ref)


def down_kernel(one_ref, two_ref, da_ref, db_ref, dc_ref, dd_ref, out_ref):
    half = da_ref.shape[0]
    one, two = one_ref[...], two_ref[...]
    out_ref[:, :half] = (nt(one, da_ref[...]) + nt(two, dc_ref[...])).astype(LOW)
    out_ref[:, half:] = (nt(one, db_ref[...]) + nt(two, dd_ref[...])).astype(LOW)


def back_kernel(
    normed_ref, mine_ref, theirs_ref, up_rows_ref, gate1_ref, up1_ref, gate2_ref, up2_ref,
    gain1_ref, gain2_ref, da_ref, db_ref, dc_ref, dd_ref,
    ga_ref, gb_ref, ua_ref, ub_ref, gc_ref, gd_ref, uc_ref, ud_ref,
    out_ref, grad_ref, low_ref, gg1_ref, ug1_ref, gg2_ref, ug2_ref, mid_ref, sum_ref,
):
    half = da_ref.shape[0]
    residual = normed_ref[...] * gain1_ref[...] + add(mine_ref[...], theirs_ref[...])
    inv = rms_scale(residual)
    normed = residual * inv
    gain = gain2_ref[...]
    out_ref[...] = (normed * gain).astype(LOW)
    upstream = up_rows_ref[...].astype(FULL)
    column_sum(sum_ref, upstream * normed)
    grad = norm_back(upstream * gain, normed, inv)
    low = grad.astype(LOW)
    grad_ref[...] = grad
    low_ref[...] = low
    first, second = low[:, :half], low[:, half:]

    def hidden_grads(da_ref, db_ref, gate_ref, up_ref, gg_ref, ug_ref):
        act_grad = nn(first, da_ref[...]) + nn(second, db_ref[...])
        gate = gate_ref[...]
        sig = jax.nn.sigmoid(gate)
        gg = (act_grad * up_ref[...] * (sig * (1.0 + gate * (1.0 - sig)))).astype(LOW)
        ug = (act_grad * (gate * sig)).astype(LOW)
        gg_ref[...] = gg
        ug_ref[...] = ug
        return gg, ug

    gg1, ug1 = hidden_grads(da_ref, db_ref, gate1_ref, up1_ref, gg1_ref, ug1_ref)
    gg2, ug2 = hidden_grads(dc_ref, dd_ref, gate2_ref, up2_ref, gg2_ref, ug2_ref)
    mid_ref[:, :half] = (
        nt(gg1, ga_ref[...]) + nt(ug1, ua_ref[...]) + nt(gg2, gc_ref[...]) + nt(ug2, uc_ref[...])
    ).astype(LOW)
    mid_ref[:, half:] = (
        nt(gg1, gb_ref[...]) + nt(ug1, ub_ref[...]) + nt(gg2, gd_ref[...]) + nt(ug2, ud_ref[...])
    ).astype(LOW)


def leave_kernel(
    grad_two_ref, mine_ref, theirs_ref, normed_ref, inv_ref,
    gain_ref, voa_ref, vob_ref, voc_ref, vod_ref,
    grad_ref, low_ref, ctx1_ref, ctx2_ref, sum_ref,
):
    half = voa_ref.shape[0]
    width = ctx1_ref.shape[1]
    hidden_grad = grad_two_ref[...] + add(mine_ref[...], theirs_ref[...])
    normed = normed_ref[...]
    column_sum(sum_ref, hidden_grad * normed)
    grad = norm_back(hidden_grad * gain_ref[...], normed, inv_ref[...])
    low = grad.astype(LOW)
    grad_ref[...] = grad
    low_ref[...] = low
    first, second = low[:, :half], low[:, half:]
    ctx1_ref[...] = (nn(first, voa_ref[:, width:]) + nn(second, vob_ref[:, width:])).astype(LOW)
    ctx2_ref[...] = (nn(first, voc_ref[:, width:]) + nn(second, vod_ref[:, width:])).astype(LOW)


def input_kernel(
    qk1_ref, v1_ref, qk2_ref, v2_ref,
    qka_ref, qkb_ref, qkc_ref, qkd_ref, voa_ref, vob_ref, voc_ref, vod_ref,
    full_ref, low_ref,
):
    half = qka_ref.shape[0]
    width = v1_ref.shape[1]
    qk1, v1, qk2, v2 = qk1_ref[...], v1_ref[...], qk2_ref[...], v2_ref[...]
    first = (
        nt(qk1, qka_ref[...]) + nt(v1, voa_ref[:, :width])
        + nt(qk2, qkc_ref[...]) + nt(v2, voc_ref[:, :width])
    )
    second = (
        nt(qk1, qkb_ref[...]) + nt(v1, vob_ref[:, :width])
        + nt(qk2, qkd_ref[...]) + nt(v2, vod_ref[:, :width])
    )
    full_ref[:, :half] = first
    full_ref[:, half:] = second
    low_ref[:, :half] = first.astype(LOW)
    low_ref[:, half:] = second.astype(LOW)


def rope_tables():
    half = HD // 2
    lane = jnp.arange(128) % HD
    freq = jnp.exp(-jnp.log(10000.0) * (lane % half).astype(FULL) / half)
    angle = jnp.arange(L, dtype=FULL)[:, None] * freq[None, :]
    return jnp.cos(angle), jnp.where(lane < half, -1.0, 1.0)[None, :] * jnp.sin(angle)


def adam_update(weight, first, second, grad, ratio, rate, decay):
    clipped = grad * ratio
    first_new = AVERAGING * first + (1.0 - AVERAGING) * clipped
    second_new = AVERAGING * second + (1.0 - AVERAGING) * clipped * clipped
    correction = 1.0 - AVERAGING**ADAM_STEP
    step = first_new / correction / (jnp.sqrt(second_new / correction) + 1e-08)
    return (weight - rate * (step + decay * weight), first_new, second_new)


def tn(rows, grads):
    out = lax.dot_general(rows, grads, (((0,), (0,)), ((), ())), preferred_element_type=FULL)
    return out.astype(LOW)


def per_device(
    layer_input, layer_cotangent,
    attend_weight, attend_first, attend_second,
    output_weight, output_first, output_second,
    gated_weight, gated_first, gated_second,
    down_weight, down_first, down_second,
    norm_gains, gains_first, gains_second,
):
    rows = layer_input.shape[0]
    wide = lax.axis_size("wide")
    block = D // wide
    me = lax.axis_index("wide")
    narrow = lax.axis_index("narrow")
    core = narrow % 2
    cols = attend_weight.shape[2]

    bits = wide_bits()
    near = bits[:-1]
    half = D // 2
    hid = down_weight.shape[0]

    attend_low = attend_weight.astype(LOW)
    att = jnp.concatenate(
        [attend_low[0], attend_low[1], attend_low[2], output_weight.T.astype(LOW)], axis=1
    )
    gu = jnp.concatenate([gated_weight[0], gated_weight[1]], axis=1).astype(LOW)
    down = down_weight.T.astype(LOW)

    order = me ^ jnp.array(block_masks(), jnp.int32)
    source = (order[:, None] * block + jnp.arange(block)[None, :]).reshape(1, D)
    mover = (lax.broadcasted_iota(jnp.int32, (D, D), 0) == source).astype(LOW)

    def whole_sequence(own):
        moved = jnp.dot(own, mover, preferred_element_type=FULL).astype(LOW)
        received = swap(moved, "narrow", 1)
        return jnp.where(
            core == 0,
            jnp.concatenate([moved, received], axis=0),
            jnp.concatenate([received, moved], axis=0),
        )

    def own_rows(value):
        return lax.dynamic_slice_in_dim(value, core * rows, rows, axis=0)

    first = widen(att, near[:1])
    gu = widen(after(gu, first), near[:1])
    att = widen(first, near[1:])
    att_y = swap(att, "wide", 1)
    att_x = swap(att, "narrow", 2)
    gu = widen(after(gu, att), near[1:])
    down = widen(after(down, att), near[:1])
    gains = norm_gains.astype(LOW).astype(FULL)[None]
    gains = widen(after(gains, att), bits)
    gains = gains.transpose(1, 0, 2).reshape(2, 1, D)
    inputs = whole_sequence(layer_input)
    upstream = whole_sequence(layer_cotangent)
    cosine, sine = rope_tables()

    inputs, att, att_y, att_x, gu, down, gains, upstream, cosine, sine = lax.optimization_barrier(
        (inputs, att, att_y, att_x, gu, down, gains, upstream, cosine, sine)
    )
    pair = 2 * cols
    qk_corner = swap(att_y[:, :pair], "narrow", 2)
    vo_corner = swap(att_x[:, pair:], "wide", 1)
    gu_y = swap(gu, "wide", 1)
    gu_x = swap(gu, "narrow", 2)
    down = widen(down, near[1:])
    qk = [[(att, pair, 0), (att_y, pair, 0)], [(att_x, pair, 0), qk_corner]]
    vo = [[(att, pair, 1), (att_y, pair, 1)], [(att_x, pair, 1), vo_corner]]
    saved = [attend_forward(inputs, qk[0], vo[0], cosine, sine)]
    second_in = after(inputs, saved[0][3], down)
    saved.append(attend_forward(second_in, qk[1], vo[1], cosine, sine))
    context = [s[3] for s in saved]

    gu_y, gu_x, context, down = lax.optimization_barrier((gu_y, gu_x, context, down))
    gate_corner = swap(gu_y[:, :hid], "narrow", 2)
    up_corner = swap(gu_x[:, hid:], "wide", 1)
    down_y = swap(down, "wide", 1)
    down_x = swap(down, "narrow", 2)
    gate_w = [[(gu, hid, 0), (gu_y, hid, 0)], [(gu_x, hid, 0), gate_corner]]
    up_w = [[(gu, hid, 1), (gu_y, hid, 1)], [(gu_x, hid, 1), up_corner]]
    (attn_part,) = by_rows(
        project_kernel, "project", 1.3e9, context, vo[0] + vo[1], [(D, LOW)]
    )
    attn_other = swap(attn_part, "narrow", 1)
    flow = [(hid, FULL), (hid, FULL), (hid, LOW)]
    normed_one, inv_one, hidden_low, gate1, up1, act1 = by_rows(
        enter_kernel, "enter", 2e9, [inputs, attn_part, attn_other],
        [gains[0], *gate_w[0], *up_w[0]], [(D, FULL), (1, FULL), (D, LOW)] + flow,
    )
    down_y, down_x, hidden_low = lax.optimization_barrier((down_y, down_x, hidden_low))
    down_corner = swap(down_y, "narrow", 2)
    gate2, up2, act2 = by_rows(
        more_kernel, "more", 2e9, [hidden_low], [*gate_w[1], *up_w[1]], flow
    )
    down_w = [down, down_y, down_x, down_corner]
    (ffn_part,) = by_rows(down_kernel, "down", 2e9, [act1, act2], down_w, [(D, LOW)])
    ffn_other = swap(ffn_part, "narrow", 1)

    (
        layer_output, grad_two, grad_two_low, gg1, ug1, gg2, ug2, mid_part, gain_two_grad,
    ) = by_rows(
        back_kernel, "back", 6e9,
        [normed_one, ffn_part, ffn_other, upstream, gate1, up1, gate2, up2],
        [gains[0], gains[1], *down_w, *gate_w[0], *up_w[0], *gate_w[1], *up_w[1]],
        [(D, LOW), (D, FULL), (D, LOW)] + [(hid, LOW)] * 4 + [(D, LOW)], sums=1,
    )
    mid_other = swap(mid_part, "narrow", 1)
    ha, hb = hidden_low[:, :half], hidden_low[:, half:]
    down_x = swap(tn(grad_two_low, act2), "narrow", 2)
    gate_y1 = swap(tn(hb, gg1), "wide", 1)
    gate_y2 = swap(tn(hb, gg2), "wide", 1)
    up_x = swap(tn(hidden_low, ug2), "narrow", 2)
    down_own = tn(grad_two_low, act1)
    gate_1, gate_2 = tn(ha, gg1), tn(ha, gg2)
    up_own = tn(hidden_low, ug1)
    mid_part, mid_other, down_own, gate_1, gate_2, up_own = lax.optimization_barrier(
        (mid_part, mid_other, down_own, gate_1, gate_2, up_own)
    )
    grad_one, grad_one_low, dctx1, dctx2, gain_one_grad = by_rows(
        leave_kernel, "leave", 2e9, [grad_two, mid_part, mid_other, normed_one, inv_one],
        [gains[0], *vo[0], *vo[1]],
        [(D, FULL), (D, LOW), (context[0].shape[1], LOW), (context[0].shape[1], LOW)], sums=1,
    )

    q, k, v, _, lse = saved[1]
    dqk2, dv2 = attend_backward(q, k, v, lse, dctx2, cosine, sine)
    xa, xb = inputs[:, :half], inputs[:, half:]
    d_out2 = tn(grad_one_low, context[1])
    vo2 = jnp.concatenate([tn(inputs, dv2), d_out2], axis=1)
    vo_x = swap(vo2, "narrow", 2)
    qk_y2 = swap(tn(xb, dqk2), "wide", 1)
    qk_2 = tn(xa, dqk2)
    down_sum = add(down_own, down_x)
    gate_sum1, gate_sum2 = add(gate_1, gate_y1), add(gate_2, gate_y2)
    dctx1, down_sum, gate_sum1, gate_sum2, qk_2 = lax.optimization_barrier(
        (dctx1, down_sum, gate_sum1, gate_sum2, qk_2)
    )
    down_y = swap(down_sum[half:].astype(LOW), "wide", 1)
    gate_x = swap(gate_sum2.astype(LOW), "narrow", 2)
    q, k, v, _, lse = saved[0]
    dqk1, dv1 = attend_backward(q, k, v, lse, dctx1, cosine, sine)
    qk_y1 = swap(tn(xb, dqk1), "wide", 1)
    vo1 = jnp.concatenate([tn(inputs, dv1), tn(grad_one_low, context[0])], axis=1)
    qk_1 = tn(xa, dqk1)

    up_sum = add(up_own, up_x)
    up_y = swap(up_sum[half:].astype(LOW), "wide", 1)
    back = near[::-1]
    down_red = narrow_down(add(down_sum[:half], down_y), back)
    gate_red = narrow_down(add(gate_sum1, gate_x), back)
    vo_sum = add(vo1, vo_x)
    vo_y = swap(vo_sum[half:].astype(LOW), "wide", 1)
    qk_sum = add(qk_1, qk_y1)
    qk_x = swap(add(qk_2, qk_y2).astype(LOW), "narrow", 2)
    up_red = narrow_down(add(up_sum[:half], up_y), back)
    last = jnp.concatenate([add(qk_sum, qk_x), add(vo_sum[:half], vo_y)], axis=1)
    att_red = narrow_down(last, back)

    gain_red = jnp.concatenate([gain_one_grad, gain_two_grad], axis=0).reshape(2, wide, block)
    gain_red = gain_red.transpose(1, 0, 2)
    gain_red = gain_red + swap(gain_red, "narrow", 2)
    for bit in bits[::-1]:
        part = gain_red.shape[0] // 2
        gain_red = gain_red[:part] + swap(gain_red[part:], "wide", bit)
    gain_red = gain_red[0]

    part_full, part_low = by_rows(
        input_kernel, "inputs", 2e9, [dqk1, dv1, dqk2, dv2],
        qk[0] + qk[1] + vo[0] + vo[1], [(D, FULL), (D, LOW)],
    )
    theirs = lax.dynamic_slice_in_dim(part_low, (1 - core) * rows, rows, axis=0)
    input_grad = own_rows(grad_one) + own_rows(part_full) + swap(theirs, "narrow", 1).astype(FULL)
    input_grad = lax.dot_general(
        input_grad, mover.astype(FULL), (((1,), (1,)), ((), ())),
        precision=lax.Precision.HIGHEST, preferred_element_type=FULL,
    )
    layer_output = nt(own_rows(layer_output), mover).astype(LOW)

    square = sum(jnp.sum(g * g) for g in (att_red, gate_red, up_red, down_red))
    square = square + jnp.where(narrow == 0, jnp.sum(gain_red * gain_red), 0.0)
    total = tree_sum(jnp.full((1, 128), square, FULL), "narrow")
    total = tree_sum(total, "wide")[0, 0]
    grad_norm = jnp.sqrt(total)
    all_tokens = rows * wide * lax.axis_size("narrow")
    clip = 0.02 * math.sqrt(all_tokens * (4 * D * D + 3 * D * FF + 2 * D))
    ratio = clip / jnp.maximum(grad_norm, clip)
    attend_red = jnp.stack([att_red[:, k * cols : (k + 1) * cols] for k in range(3)])
    output_red = att_red[:, 3 * cols :].T
    gated_red = jnp.stack([gate_red, up_red])
    new_attend = adam_update(
        attend_weight, attend_first, attend_second, attend_red, ratio, D ** (-0.5), WEIGHT_DECAY
    )
    new_output = adam_update(
        output_weight, output_first, output_second, output_red, ratio,
        max(D // 64, 1) ** (-0.5), WEIGHT_DECAY,
    )
    new_gated = adam_update(
        gated_weight, gated_first, gated_second, gated_red, ratio, D ** (-0.5), WEIGHT_DECAY
    )
    new_down = adam_update(
        down_weight, down_first, down_second, down_red.T, ratio, FF ** (-0.5), WEIGHT_DECAY
    )
    new_gains = adam_update(norm_gains, gains_first, gains_second, gain_red, ratio, 0.4, 0.0)
    return (
        layer_output, input_grad, grad_norm,
        *new_attend, *new_output, *new_gated, *new_down, *new_gains,
    )


def solution(mesh):
    rows = P(("wide", "narrow"), None)
    stacked = P(None, "wide", "narrow")
    turned = P("narrow", "wide")
    gains = P(None, "wide")
    params = (stacked,) * 3 + (turned,) * 3 + (stacked,) * 3 + (turned,) * 3 + (gains,) * 3
    return jax.shard_map(
        per_device,
        mesh=mesh,
        in_specs=(rows, rows) + params,
        out_specs=(rows, rows, P()) + params,
        check_vma=False,
    )
```

profile of v0, /device:TPU:0, one launch (start us, length us, event | category | flops | bytes accessed | tf_op | source)
XLA Modules:
  0.0 319.2 jit_solution(3846994136488676343)
XLA Ops:
  2.8 4.1 %collective-permute-start.1 = (bf16[96,768]{1,0:T(8,128)(2,1)S(1)}, bf16[96,768]{1,0:T(8,128)(2,1)S(1)}, u32[]{:S(2)}, u32[]{:S(2)}) collective-permute-start(bf16[96,768]{1,0:T(8,128)(2,1)S(1)} %pad_maximum_fusion.8), channel_id=1, source_target_pairs={{0,16},{4,20},{8,24},{12,28},{16,0},{20,4},{24,8},{28,12},{1,17},{... | collective-permute-start | bytes 442376 | tf_op jit(solution)/shard_map/ppermute | solution.py:29
  10.3 3.7 %collective-permute-done.1 = bf16[96,768]{1,0:T(8,128)(2,1)S(1)} collective-permute-done((bf16[96,768]{1,0:T(8,128)(2,1)S(1)}, bf16[96,768]{1,0:T(8,128)(2,1)S(1)}, u32[]{:S(2)}, u32[]{:S(2)}) %collective-permute-start.1) | collective-permute-done | bytes 147488 | tf_op jit(solution)/shard_map/ppermute | solution.py:29
  18.2 4.1 %collective-permute-done.2 = bf16[192,768]{1,0:T(8,128)(2,1)S(1)} collective-permute-done((bf16[192,768]{1,0:T(8,128)(2,1)S(1)}, bf16[192,768]{1,0:T(8,128)(2,1)S(1)}, u32[]{:S(2)}, u32[]{:S(2)}) %collective-permute-start.2) | collective-permute-done | bytes 294944 | tf_op jit(solution)/shard_map/ppermute | solution.py:29
  32.3 4.5 %collective-permute-done.5 = bf16[96,1024]{1,0:T(8,128)(2,1)S(1)} collective-permute-done((bf16[96,1024]{1,0:T(8,128)(2,1)S(1)}, bf16[96,1024]{1,0:T(8,128)(2,1)S(1)}, u32[]{:S(2)}, u32[]{:S(2)}) %collective-permute-start.5) | collective-permute-done | bytes 196640 | tf_op jit(solution)/shard_map/ppermute | solution.py:29
  40.0 5.6 %collective-permute-done.7 = bf16[96,512]{1,0:T(8,128)(2,1)S(1)} collective-permute-done((bf16[96,512]{1,0:T(8,128)(2,1)S(1)}, bf16[96,512]{1,0:T(8,128)(2,1)S(1)}, u32[]{:S(2)}, u32[]{:S(2)}) %collective-permute-start.7) | collective-permute-done | bytes 98336 | tf_op jit(solution)/shard_map/ppermute | solution.py:29
  50.9 5.0 %collective-permute-done.6 = bf16[192,1024]{1,0:T(8,128)(2,1)S(1)} collective-permute-done((bf16[192,1024]{1,0:T(8,128)(2,1)S(1)}, bf16[192,1024]{1,0:T(8,128)(2,1)S(1)}, u32[]{:S(2)}, u32[]{:S(2)}) %collective-permute-start.6) | collective-permute-done | bytes 393248 | tf_op jit(solution)/shard_map/ppermute | solution.py:29
  62.6 9.8 %attend_forward.2 = (bf16[3,1024,64]{2,1,0:T(8,128)(2,1)S(1)}, bf16[3,1024,64]{2,1,0:T(8,128)(2,1)S(1)}, bf16[3,1024,64]{2,1,0:T(8,128)(2,1)S(1)}, bf16[1024,192]{1,0:T(8,128)(2,1)S(1)}, f32[3,1,1024]{2,1,0:T(1,128)S(1)}) custom-call(bf16[1024,768]{1,0:T(8,128)(2,1)S(1)} %maximum_select_fusion.rows_ref, bf16[384,768]{1,0:T(8,128)(2,1)S(1)} %copy-done.7, ...), custom_call_target="tpu_custom_call" | custom-call | flops 8000000000 | bytes 8388608 | tf_op jit(solution)/shard_map/attend_forward/pallas_call | solution.py:177
  74.2 6.1 %collective-permute-done.15.qkb_ref.qkd_ref = bf16[384,384]{1,0:T(8,128)(2,1)S(1)} collective-permute-done((bf16[384,384]{1,0:T(8,128)(2,1)S(1)}, bf16[384,384]{1,0:T(8,128)(2,1)S(1)}, u32[]{:S(2)}, u32[]{:S(2)}) %collective-permute-start.15) | collective-permute-done | bytes 294944 | tf_op jit(solution)/shard_map/ppermute | solution.py:29
  80.4 10.0 %attend_forward.3 = (bf16[3,1024,64]{2,1,0:T(8,128)(2,1)S(1)}, bf16[3,1024,64]{2,1,0:T(8,128)(2,1)S(1)}, bf16[3,1024,64]{2,1,0:T(8,128)(2,1)S(1)}, bf16[1024,192]{1,0:T(8,128)(2,1)S(1)}, f32[3,1,1024]{2,1,0:T(1,128)S(1)}) custom-call(bf16[1024,768]{1,0:T(8,128)(2,1)S(1)} %maximum_select_fusion.rows_ref, ...), custom_call_target="tpu_custom_call" | custom-call | flops 8000000000 | bytes 8388608 | tf_op jit(solution)/shard_map/attend_forward/pallas_call | solution.py:177
  93.8 3.6 %project.1.mine_ref = bf16[1024,768]{1,0:T(8,128)(2,1)S(1)} custom-call(bf16[1024,192]{1,0:T(8,128)(2,1)S(1)} %get-tuple-element.106.one_ref, bf16[1024,192]{1,0:T(8,128)(2,1)S(1)} %get-tuple-element.107.two_ref, bf16[384,768]{1,0:T(8,128)(2,1)S(1)} %copy-done.7, bf16[384,768]{1,0:T(8,128)(2,1)} %collective-permute-done.3.qkb_ref.vob_ref, ...), custom_call_target="tpu_custom_call" | custom-call | flops 1300000000 | bytes 16777216 | tf_op jit(solution)/shard_map/project/pallas_call | solution.py:272
  103.0 6.8 %enter.1 = (f32[1024,768]{1,0:T(8,128)}, f32[1024,1]{1,0:T(8,128)S(1)}, bf16[1024,768]{1,0:T(8,128)(2,1)S(1)}, f32[1024,512]{1,0:T(8,128)}, f32[1024,512]{1,0:T(8,128)}, /*index=5*/bf16[1024,512]{1,0:T(8,128)(2,1)S(1)}) custom-call(bf16[1024,768]{1,0:T(8,128)(2,1)} %copy-done.2, bf16[1024,768]{1,0:T(8,128)(2,1)} %copy-done.9, bf16[1024,768]{1,0:T(8,128)(2,1)} %copy-done.63, ...), custom_call_target="tpu_custom_call" | custom-call | flops 2000000000 | bytes 16777216 | tf_op jit(solution)/shard_map/enter/pallas_call | solution.py:272
  111.5 8.1 %collective-permute-done.20.gb_ref.gd_ref = bf16[384,512]{1,0:T(8,128)(2,1)S(1)} collective-permute-done((bf16[384,512]{1,0:T(8,128)(2,1)S(1)}, bf16[384,512]{1,0:T(8,128)(2,1)S(1)}, u32[]{:S(2)}, u32[]{:S(2)}) %collective-permute-start.20) | collective-permute-done | bytes 393248 | tf_op jit(solution)/shard_map/ppermute | solution.py:29
  119.7 4.0 %more.1 = (f32[1024,512]{1,0:T(8,128)}, f32[1024,512]{1,0:T(8,128)}, bf16[1024,512]{1,0:T(8,128)(2,1)S(1)}) custom-call(bf16[1024,768]{1,0:T(8,128)(2,1)S(1)} %get-tuple-element.114.hidden_ref, bf16[384,1024]{1,0:T(8,128)(2,1)S(1)} %collective-permute-done.13.ga_ref.ua_ref.gc_ref.uc_ref, bf16[384,512]{1,0:T(8,128)(2,1)S(1)} %collective-permute-done.20.gb_ref.gd_ref, ...), custom_call_target="tpu_custom_call" | custom-call | flops 2000000000 | bytes 16777216 | tf_op jit(solution)/shard_map/more/pallas_call | solution.py:272
  127.3 3.7 %down.1.mine_ref = bf16[1024,768]{1,0:T(8,128)(2,1)} custom-call(bf16[1024,512]{1,0:T(8,128)(2,1)S(1)} %get-tuple-element.111.one_ref, bf16[1024,512]{1,0:T(8,128)(2,1)S(1)} %get-tuple-element.116.two_ref, bf16[384,512]{1,0:T(8,128)(2,1)S(1)} %constant_dynamic-update-slice_fusion.da_ref, bf16[384,512]{1,0:T(8,128)(2,1)S(1)} %collective-permute-done.18.db_ref, ...), custom_call_target="tpu_custom_call" | custom-call | flops 2000000000 | bytes 16777216 | tf_op jit(solution)/shard_map/down/pallas_call | solution.py:272
  131.0 3.7 %collective-permute-done.23.theirs_ref = bf16[1024,768]{1,0:T(8,128)(2,1)} collective-permute-done((bf16[1024,768]{1,0:T(8,128)(2,1)}, bf16[1024,768]{1,0:T(8,128)(2,1)}, u32[]{:S(2)}, u32[]{:S(2)}) %collective-permute-start.23) | collective-permute-done | bytes 1572896 | tf_op jit(solution)/shard_map/ppermute | solution.py:29
  137.8 13.3 %back.1 = (bf16[1024,768]{1,0:T(8,128)(2,1)}, f32[1024,768]{1,0:T(8,128)}, bf16[1024,768]{1,0:T(8,128)(2,1)}, bf16[1024,512]{1,0:T(8,128)(2,1)S(1)}, bf16[1024,5...) custom-call(f32[1024,768]{1,0:T(8,128)} %get-tuple-element.110.norme, ...), custom_call_target="tpu_custom_call" | custom-call | flops 6000000000 | bytes 16777216 | tf_op jit(solution)/shard_map/back/pallas_call | solution.py:272
  170.8 7.7 %leave.1 = (f32[1024,768]{1,0:T(8,128)}, bf16[1024,768]{1,0:T(8,128)(2,1)S(1)}, bf16[1024,192]{1,0:T(8,128)(2,1)S(1)}, bf16[1024,192]{1,0:T(8,128)(2,1)S(1)}, f32[1,768]{1,0:T(1,128)S(1)}) custom-call(f32[1024,768]{1,0:T(8,128)} %get-tuple-element.125.grad_two_ref, bf16[1024,768]{1,0:T(8,128)(2,1)} %get-tuple-element.131.mine_ref, ...), custom_call_target="tpu_custom_call" | custom-call | flops 2000000000 | bytes 16777216 | tf_op jit(solution)/shard_map/leave/pallas_call | solution.py:272
  183.2 9.7 %attend_backward.2 = (bf16[1024,384]{1,0:T(8,128)(2,1)S(1)}, bf16[1024,192]{1,0:T(8,128)(2,1)S(1)}) custom-call(bf16[3,1024,64]{2,1,0:T(8,128)(2,1)S(1)} %copy-done.49, bf16[3,1024,64]{2,1,0:T(8,128)(2,1)S(1)} %copy-done.51, bf16[3,1024,64]{2,1,0:T(8,128)(2,1)S(1)} %copy-done.53, f32[3,1,1024]{2,1,0:T(1,128)S(1)} %copy-done.57, ...), custom_call_target="tpu_custom_call" | custom-call | flops 8999999488 | bytes 8388608 | tf_op jit(solution)/shard_map/attend_backward/pallas_call | solution.py:245
  210.5 9.5 %attend_backward.3 = (bf16[1024,384]{1,0:T(8,128)(2,1)S(1)}, bf16[1024,192]{1,0:T(8,128)(2,1)S(1)}) custom-call(bf16[3,1024,64]{2,1,0:T(8,128)(2,1)S(1)} %copy-done.43, bf16[3,1024,64]{2,1,0:T(8,128)(2,1)S(1)} %copy-done.45, bf16[3,1024,64]{2,1,0:T(8,128)(2,1)S(1)} %copy-done.47, f32[3,1,1024]{2,1,0:T(1,128)S(1)} %copy-done.55, ...), custom_call_target="tpu_custom_call" | custom-call | flops 8999999488 | bytes 8388608 | tf_op jit(solution)/shard_map/attend_backward/pallas_call | solution.py:245
  225.3 6.3 %inputs.1 = (f32[1024,768]{1,0:T(8,128)}, bf16[1024,768]{1,0:T(8,128)(2,1)}) custom-call(bf16[1024,384]{1,0:T(8,128)(2,1)S(1)} %get-tuple-element.150.qk1_ref, bf16[1024,192]{1,0:T(8,128)(2,1)S(1)} %get-tuple-element.151.v1_ref, bf16[1024,384]{1,0:T(8,128)(2,1)S(1)} %get-tuple-element.148.qk2_ref, bf16[1024,192]{1,0:T(8,128)(2,1)S(1)} %get-tuple-element.152.v2_ref, ...), custom_call_target="tpu_custom_call" | custom-call | flops 2000000000 | bytes 16777216 | tf_op jit(solution)/shard_map/inputs/pallas_call | solution.py:272
  250.5 6.4 %collective-permute-done.31 = bf16[384,384]{0,1:T(8,128)(2,1)S(1)} collective-permute-done((bf16[384,384]{0,1:T(8,128)(2,1)S(1)}, bf16[384,384]{0,1:T(8,128)(2,1)S(1)}, u32[]{:S(2)}, u32[]{:S(2)}) %collective-permute-start.31) | collective-permute-done | bytes 294944 | tf_op jit(solution)/shard_map/ppermute | solution.py:29
  271.7 6.3 %collective-permute-done.34 = bf16[192,768]{0,1:T(8,128)(2,1)S(1)} collective-permute-done((bf16[192,768]{0,1:T(8,128)(2,1)S(1)}, bf16[192,768]{0,1:T(8,128)(2,1)S(1)}, u32[]{:S(2)}, u32[]{:S(2)}) %collective-permute-start.34) | collective-permute-done | bytes 294944 | tf_op jit(solution)/shard_map/ppermute | solution.py:29
  279.6 7.2 %collective-permute-done.35 = bf16[96,768]{0,1:T(8,128)(2,1)S(1)} collective-permute-done((bf16[96,768]{0,1:T(8,128)(2,1)S(1)}, bf16[96,768]{0,1:T(8,128)(2,1)S(1)}, u32[]{:S(2)}, u32[]{:S(2)}) %collective-permute-start.35) | collective-permute-done | bytes 147488 | tf_op jit(solution)/shard_map/ppermute | solution.py:29
  300.3 5.2 %fusion = f32[512,768]{1,0:T(8,128)} fusion(bf16[512,768]{1,0:T(8,128)(2,1)} %collective-permute-done.28, f32[1024,768]{1,0:T(8,128)} %get-tuple-element.153, s32[]{:T(128)S(6)} %select_n.71, f32[1024,768]{1,0:T(8,128)S(1)} %copy-done.68, s32[768]{0:T(1024)S(1)} %copy-done.88), kind=kOutput, calls=%fused_computation.1 | convolution fusion | flops 3625648128 | bytes 5509124 | tf_op jit(solution)/shard_map/dot_general | solution.py:621
  (405 shorter events, 157.8 us)
Async XLA Ops:
  8.7 37.0 %collective-permute-start.11 = (bf16[512,768]{1,0:T(8,128)(2,1)S(1)}, bf16[512,768]{1,0:T(8,128)(2,1)}, u32[]{:S(2)}, u32[]{:S(2)}) collective-permute-start(bf16[512,768]{1,0:T(8,128)(2,1)S(1)} %fusion.12), channel_id=1, source_target_pairs={{0,1},{1,0},{2,3},{3,2},{4,5},{5,4},{6,7},{7,6},{8,9},{9,8},{10,11... | collective-permute-start | bytes 2359304 | tf_op jit(solution)/shard_map/ppermute | solution.py:29
  9.8 39.0 %collective-permute-start = (bf16[512,768]{1,0:T(8,128)(2,1)S(1)}, bf16[512,768]{1,0:T(8,128)(2,1)}, u32[]{:S(2)}, u32[]{:S(2)}) collective-permute-start(bf16[512,768]{1,0:T(8,128)(2,1)S(1)} %fusion.13), channel_id=1, source_target_pairs={{0,1},{1,0},{2,3},{3,2},{4,5},{5,4},{6,7},{7,6},{8,9},{9,8},{10,11... | collective-permute-start | bytes 2359304 | tf_op jit(solution)/shard_map/ppermute | solution.py:29
  36.8 19.2 %collective-permute-start.3 = (bf16[384,768]{1,0:T(8,128)(2,1)S(1)}, bf16[384,768]{1,0:T(8,128)(2,1)}, u32[]{:S(2)}, u32[]{:S(2)}) collective-permute-start(bf16[384,768]{1,0:T(8,128)(2,1)S(1)} %pad_maximum_fusion.2.qka_ref.voa_ref), channel_id=1, source_target_pairs={{0,4},{4,0},{8,12},{12,8},{16,20},{20,16},{24,28},{28,24},{1,5},{5... | collective-permute-start | bytes 1769480 | tf_op jit(solution)/shard_map/ppermute | solution.py:29
  38.4 17.6 %collective-permute-start.4 = (bf16[384,768]{1,0:T(8,128)(2,1)S(1)}, bf16[384,768]{1,0:T(8,128)(2,1)}, u32[]{:S(2)}, u32[]{:S(2)}) collective-permute-start(bf16[384,768]{1,0:T(8,128)(2,1)S(1)} %pad_maximum_fusion.2.qka_ref.voa_ref), channel_id=1, source_target_pairs={{0,2},{1,3},{2,0},{3,1},{4,6},{5,7},{6,4},{7,5},{8,10},{9,11},{10,... | collective-permute-start | bytes 1769480 | tf_op jit(solution)/shard_map/ppermute | solution.py:29
  56.0 37.7 %collective-permute-start.12 = (bf16[384,1024]{1,0:T(8,128)(2,1)S(1)}, bf16[384,1024]{1,0:T(8,128)(2,1)S(1)}, u32[]{:S(2)}, u32[]{:S(2)}) collective-permute-start(bf16[384,1024]{1,0:T(8,128)(2,1)S(1)} %pad_maximum_fusion.1.ga_ref.ua_ref), channel_id=1, source_target_pairs={{0,4},{4,0},{8,12},{12,8},{16,20},{20,16},{24,28},{28,24},{1,5},{5... | collective-permute-start | bytes 2359304 | tf_op jit(solution)/shard_map/ppermute | solution.py:29
  56.1 37.6 %collective-permute-start.13 = (bf16[384,1024]{1,0:T(8,128)(2,1)S(1)}, bf16[384,1024]{1,0:T(8,128)(2,1)S(1)}, u32[]{:S(2)}, u32[]{:S(2)}) collective-permute-start(bf16[384,1024]{1,0:T(8,128)(2,1)S(1)} %pad_maximum_fusion.1.ga_ref.ua_ref), channel_id=1, source_target_pairs={{0,2},{1,3},{2,0},{3,1},{4,6},{5,7},{6,4},{7,5},{8,10},{9,11},{10,... | collective-permute-start | bytes 2359304 | tf_op jit(solution)/shard_map/ppermute | solution.py:29
  56.2 18.0 %collective-permute-start.14 = (bf16[192,512]{1,0:T(8,128)(2,1)S(1)}, bf16[192,512]{1,0:T(8,128)(2,1)S(1)}, u32[]{:S(2)}, u32[]{:S(2)}) collective-permute-start(bf16[192,512]{1,0:T(8,128)(2,1)S(1)} %pad_maximum_fusion.7), channel_id=1, source_target_pairs={{0,8},{4,12},{8,0},{12,4},{16,24},{20,28},{24,16},{28,20},{1,9},{5... | collective-permute-start | bytes 589832 | tf_op jit(solution)/shard_map/ppermute | solution.py:29
  57.5 22.8 %collective-permute-start.15 = (bf16[384,384]{1,0:T(8,128)(2,1)S(1)}, bf16[384,384]{1,0:T(8,128)(2,1)S(1)}, u32[]{:S(2)}, u32[]{:S(2)}) collective-permute-start(bf16[384,384]{1,0:T(8,128)(2,1)S(1)} %slice.164), channel_id=1, source_target_pairs={{0,2},{1,3},{2,0},{3,1},{4,6},{5,7},{6,4},{7,5},{8,10},{9,11},{10,... | collective-permute-start | bytes 884744 | tf_op jit(solution)/shard_map/ppermute | solution.py:29
  60.5 19.8 %collective-permute-start.16 = (bf16[384,384]{1,0:T(8,128)(2,1)S(1)}, bf16[384,384]{1,0:T(8,128)(2,1)S(1)}, u32[]{:S(2)}, u32[]{:S(2)}) collective-permute-start(bf16[384,384]{1,0:T(8,128)(2,1)S(1)} %slice.165), channel_id=1, source_target_pairs={{0,4},{4,0},{8,12},{12,8},{16,20},{20,16},{24,28},{28,24},{1,5},{5... | collective-permute-start | bytes 884744 | tf_op jit(solution)/shard_map/ppermute | solution.py:29
  99.6 20.1 %collective-permute-start.20 = (bf16[384,512]{1,0:T(8,128)(2,1)S(1)}, bf16[384,512]{1,0:T(8,128)(2,1)S(1)}, u32[]{:S(2)}, u32[]{:S(2)}) collective-permute-start(bf16[384,512]{1,0:T(8,128)(2,1)S(1)} %slice.167), channel_id=1, source_target_pairs={{0,2},{1,3},{2,0},{3,1},{4,6},{5,7},{6,4},{7,5},{8,10},{9,11},{10,... | collective-permute-start | bytes 1179656 | tf_op jit(solution)/shard_map/ppermute | solution.py:29
  101.4 18.3 %collective-permute-start.21 = (bf16[384,512]{1,0:T(8,128)(2,1)S(1)}, bf16[384,512]{1,0:T(8,128)(2,1)S(1)}, u32[]{:S(2)}, u32[]{:S(2)}) collective-permute-start(bf16[384,512]{1,0:T(8,128)(2,1)S(1)} %slice.168), channel_id=1, source_target_pairs={{0,4},{4,0},{8,12},{12,8},{16,20},{20,16},{24,28},{28,24},{1,5},{5... | collective-permute-start | bytes 1179656 | tf_op jit(solution)/shard_map/ppermute | solution.py:29
  151.1 18.6 %collective-permute-start.24 = (bf16[1024,768]{1,0:T(8,128)(2,1)}, bf16[1024,768]{1,0:T(8,128)(2,1)S(1)}, u32[]{:S(2)}, u32[]{:S(2)}) collective-permute-start(bf16[1024,768]{1,0:T(8,128)(2,1)} %get-tuple-element.131.mine_ref), channel_id=1, source_target_pairs={{0,1},{1,0},{2,3},{3,2},{4,5},{5,4},{6,7},{7,6},{8,9},{9,8},{10,11... | collective-permute-start | bytes 4718600 | tf_op jit(solution)/shard_map/ppermute | solution.py:29
  153.8 39.1 %collective-permute-start.27 = (bf16[384,512]{1,0:T(8,128)(2,1)}, bf16[384,512]{1,0:T(8,128)(2,1)}, u32[]{:S(2)}, u32[]{:S(2)}) collective-permute-start(bf16[384,512]{1,0:T(8,128)(2,1)} %convolution_convert_fusion.4), channel_id=1, source_target_pairs={{0,4},{4,0},{8,12},{12,8},{16,20},{20,16},{24,28},{28,24},{1,5},{5... | collective-permute-start | bytes 1179656 | tf_op jit(solution)/shard_map/ppermute | solution.py:29
  155.6 39.3 %collective-permute-start.26 = (bf16[384,512]{1,0:T(8,128)(2,1)}, bf16[384,512]{1,0:T(8,128)(2,1)}, u32[]{:S(2)}, u32[]{:S(2)}) collective-permute-start(bf16[384,512]{1,0:T(8,128)(2,1)} %convolution_convert_fusion.5), channel_id=1, source_target_pairs={{0,4},{4,0},{8,12},{12,8},{16,20},{20,16},{24,28},{28,24},{1,5},{5... | collective-permute-start | bytes 1179656 | tf_op jit(solution)/shard_map/ppermute | solution.py:29
  159.1 39.1 %collective-permute-start.25 = (bf16[768,512]{1,0:T(8,128)(2,1)}, bf16[768,512]{1,0:T(8,128)(2,1)}, u32[]{:S(2)}, u32[]{:S(2)}) collective-permute-start(bf16[768,512]{1,0:T(8,128)(2,1)} %convolution_convert_fusion.1), channel_id=1, source_target_pairs={{0,2},{1,3},{2,0},{3,1},{4,6},{5,7},{6,4},{7,5},{8,10},{9,11},{10,... | collective-permute-start | bytes 2359304 | tf_op jit(solution)/shard_map/ppermute | solution.py:29
  161.3 42.8 %collective-permute-start.39 = (bf16[768,512]{1,0:T(8,128)(2,1)}, bf16[768,512]{1,0:T(8,128)(2,1)}, u32[]{:S(2)}, u32[]{:S(2)}) collective-permute-start(bf16[768,512]{1,0:T(8,128)(2,1)} %convolution_convert_fusion), channel_id=1, source_target_pairs={{0,2},{1,3},{2,0},{3,1},{4,6},{5,7},{6,4},{7,5},{8,10},{9,11},{10,... | collective-permute-start | bytes 2359304 | tf_op jit(solution)/shard_map/ppermute | solution.py:29
  180.6 43.0 %collective-permute-start.46 = (f32[8,2,96]{2,1,0:T(2,128)S(1)}, f32[8,2,96]{2,1,0:T(2,128)S(1)}, u32[]{:S(2)}, u32[]{:S(2)}) collective-permute-start(f32[8,2,96]{2,1,0:T(2,128)S(1)} %bitcast.92), channel_id=1, source_target_pairs={{0,2},{1,3},{2,0},{3,1},{4,6},{5,7},{6,4},{7,5},{8,10},{9,11},{10,... | collective-permute-start | bytes 18440 | tf_op jit(solution)/shard_map/ppermute | solution.py:29
  200.4 42.4 %collective-permute-start.43 = (bf16[384,512]{1,0:T(8,128)(2,1)}, bf16[384,512]{1,0:T(8,128)(2,1)}, u32[]{:S(2)}, u32[]{:S(2)}) collective-permute-start(bf16[384,512]{1,0:T(8,128)(2,1)} %slice.327), channel_id=1, source_target_pairs={{0,4},{4,0},{8,12},{12,8},{16,20},{20,16},{24,28},{28,24},{1,5},{5... | collective-permute-start | bytes 1179656 | tf_op jit(solution)/shard_map/ppermute | solution.py:29
  207.2 36.9 %collective-permute-start.40 = (bf16[384,512]{1,0:T(8,128)(2,1)}, bf16[384,512]{1,0:T(8,128)(2,1)}, u32[]{:S(2)}, u32[]{:S(2)}) collective-permute-start(bf16[384,512]{1,0:T(8,128)(2,1)} %slice.328), channel_id=1, source_target_pairs={{0,4},{4,0},{8,12},{12,8},{16,20},{20,16},{24,28},{28,24},{1,5},{5... | collective-permute-start | bytes 1179656 | tf_op jit(solution)/shard_map/ppermute | solution.py:29
  208.7 38.4 %collective-permute-start.36 = (bf16[384,512]{1,0:T(8,128)(2,1)}, bf16[384,512]{1,0:T(8,128)(2,1)}, u32[]{:S(2)}, u32[]{:S(2)}) collective-permute-start(bf16[384,512]{1,0:T(8,128)(2,1)} %convert_add_fusion.5), channel_id=1, source_target_pairs={{0,2},{1,3},{2,0},{3,1},{4,6},{5,7},{6,4},{7,5},{8,10},{9,11},{10,... | collective-permute-start | bytes 1179656 | tf_op jit(solution)/shard_map/ppermute | solution.py:29
  223.1 18.1 %collective-permute-start.30 = (bf16[384,384]{0,1:T(8,128)(2,1)}, bf16[384,384]{0,1:T(8,128)(2,1)}, u32[]{:S(2)}, u32[]{:S(2)}) collective-permute-start(bf16[384,384]{0,1:T(8,128)(2,1)} %convolution_convert_fusion.12), channel_id=1, source_target_pairs={{0,4},{4,0},{8,12},{12,8},{16,20},{20,16},{24,28},{28,24},{1,5},{5... | collective-permute-start | bytes 884744 | tf_op jit(solution)/shard_map/ppermute | solution.py:29
  239.8 19.2 %collective-permute-start.32 = (bf16[768,384]{0,1:T(8,128)(2,1)}, bf16[768,384]{0,1:T(8,128)(2,1)}, u32[]{:S(2)}, u32[]{:S(2)}) collective-permute-start(bf16[768,384]{0,1:T(8,128)(2,1)} %pad_maximum_fusion.3), channel_id=1, source_target_pairs={{0,2},{1,3},{2,0},{3,1},{4,6},{5,7},{6,4},{7,5},{8,10},{9,11},{10,... | collective-permute-start | bytes 1769480 | tf_op jit(solution)/shard_map/ppermute | solution.py:29
  242.9 57.3 %collective-permute-start.28 = (bf16[512,768]{1,0:T(8,128)(2,1)}, bf16[512,768]{1,0:T(8,128)(2,1)}, u32[]{:S(2)}, u32[]{:S(2)}) collective-permute-start(bf16[512,768]{1,0:T(8,128)(2,1)} %constant_dynamic-slice_fusion), channel_id=1, source_target_pairs={{0,1},{1,0},{2,3},{3,2},{4,5},{5,4},{6,7},{7,6},{8,9},{9,8},{10,11... | collective-permute-start | bytes 2359304 | tf_op jit(solution)/shard_map/ppermute | solution.py:29
  261.2 17.7 %collective-permute-start.45 = (bf16[96,512]{1,0:T(8,128)(2,1)S(1)}, bf16[96,512]{1,0:T(8,128)(2,1)S(1)}, u32[]{:S(2)}, u32[]{:S(2)}) collective-permute-start(bf16[96,512]{1,0:T(8,128)(2,1)S(1)} %slice.334), channel_id=1, source_target_pairs={{0,16},{4,20},{8,24},{12,28},{16,0},{20,4},{24,8},{28,12},{1,17},{... | collective-permute-start | bytes 294920 | tf_op jit(solution)/shard_map/ppermute | solution.py:29
  (129 other events, 922.8 us)
where the time goes:
time: 323 us; the launch traced here: 319 us
  Pallas kernels  84.5 us (26%)
  waiting for transfers between devices  83.8 us (26%)
  starting transfers between devices  52.8 us (16%)
  other arithmetic  32.8 us (10%)
  matrix products  32.3 us (10%)
  local copies, waits for them, and re-layouts  26.2 us (8%)
  between operations  6.8 us (2%)
    ppermute x55, waiting for transfers between devices, swap(): return lax.ppermute(value, axis, [(i, i ^ bit) for i in range(size)])  83.8 us
    ppermute x55, starting transfers between devices, swap(): return lax.ppermute(value, axis, [(i, i ^ bit) for i in range(size)])  52.8 us
    pallas_call x7, Pallas kernels, by_rows(): pl.pallas_call(kernel, grid=(L // QB,), in_specs=specs + list(held_specs)...  45.5 us
    dot_general x16, matrix products, tn(): lax.dot_general(rows, grads, (((0,), (0,)), ((), ())), preferred_element_...  22.4 us
    pallas_call x2, Pallas kernels, attend_forward(): pl.pallas_call(attend_kernel, grid=(1,), in_specs=list(specs), out_specs=...  19.8 us
    unnamed x204, local copies, waits for them, and re-layouts  19.8 us
    pallas_call x2, Pallas kernels, attend_backward(): pl.pallas_call(attend_back_kernel, out_shape=(jax.ShapeDtypeStruct((L, 2...  19.1 us
    add x13, other arithmetic, add(): return kept.astype(FULL) + received.astype(FULL)  11.7 us
  transfers between devices with their start and end apart: 55, of which 22 were waited for; matrix products, arithmetic and copies ran while one was open for 21% of the time, Pallas kernels for 20%

commit v1 on v0

--- a/solution.py
+++ b/solution.py
@@ -60,13 +60,6 @@
         half = held.shape[0] // 2
         held = add(held[:half], swap(held[half:].astype(LOW), "wide", bit))
     return held
-
-
-def tree_sum(value, axis):
-    bits = [1 << b for b in range(lax.axis_size(axis).bit_length() - 1)]
-    for bit in bits:
-        value = value + swap(value, axis, bit)
-    return value
 
 
 def turn(value, cosine, sine, sign):
@@ -181,7 +174,7 @@
         out_specs=[whole(o) for o in outs],
         out_shape=outs,
         scratch_shapes=[pltpu.VMEM((heads, L, HD), LOW)],
-        compiler_params=pltpu.CompilerParams(vmem_limit_bytes=40 << 20),
+        compiler_params=pltpu.CompilerParams(vmem_limit_bytes=24 << 20),
         cost_estimate=pl.CostEstimate(
             flops=8 * 10**9, bytes_accessed=8 << 20, transcendentals=2 << 20
         ),
@@ -254,7 +247,7 @@
             pltpu.VMEM((heads, L, HD), FULL),
             pltpu.VMEM((heads, L, HD), FULL),
         ],
-        compiler_params=pltpu.CompilerParams(vmem_limit_bytes=40 << 20),
+        compiler_params=pltpu.CompilerParams(vmem_limit_bytes=24 << 20),
         cost_estimate=pl.CostEstimate(
             flops=9 * 10**9, bytes_accessed=8 << 20, transcendentals=2 << 20
         ),
@@ -262,9 +255,12 @@
     )(q, k, v, lse, dctx, cosine, sine)
 
 
-def by_rows(kernel, name, flops, row_args, fixed, outs, sums=0):
+def held_once(array):
+    return pl.BlockSpec(array.shape, lambda i: (0, 0), pipeline_mode=pl.Buffered(1))
+
+
+def by_rows(kernel, name, flops, row_args, fixed, outs, sums=0, scratch=()):
     specs = [pl.BlockSpec((QB, r.shape[1]), lambda i: (i, 0)) for r in row_args]
-    held, held_specs = zip(*[columns(p) for p in fixed])
     shapes = [jax.ShapeDtypeStruct((L, w), t) for w, t in outs]
     out_specs = [pl.BlockSpec((QB, w), lambda i: (i, 0)) for w, _ in outs]
     shapes += [jax.ShapeDtypeStruct((1, D), FULL)] * sums
@@ -272,15 +268,16 @@
     return pl.pallas_call(
         kernel,
         grid=(L // QB,),
-        in_specs=specs + list(held_specs),
+        in_specs=specs + [held_once(f) for f in fixed],
         out_specs=out_specs,
         out_shape=shapes,
-        compiler_params=pltpu.CompilerParams(vmem_limit_bytes=48 << 20),
+        scratch_shapes=list(scratch),
+        compiler_params=pltpu.CompilerParams(vmem_limit_bytes=30 << 20),
         cost_estimate=pl.CostEstimate(
             flops=int(flops), bytes_accessed=16 << 20, transcendentals=1 << 20
         ),
         name=name,
-    )(*row_args, *held)
+    )(*row_args, *fixed)
 
 
 def rms_scale(residual):
@@ -299,26 +296,64 @@
     sum_ref[...] += jnp.sum(value, axis=0, keepdims=True)
 
 
-def project_kernel(one_ref, two_ref, voa_ref, vob_ref, voc_ref, vod_ref, out_ref):
-    width = one_ref.shape[1]
-    half = voa_ref.shape[0]
+def heads_out(held_ref, refs):
+    att_ref, y_ref, x_ref, corner_ref = refs
+    width = held_ref.shape[2]
+
+    @pl.when(pl.program_id(0) == 0)
+    def _():
+        for p, ref in enumerate((att_ref, y_ref, x_ref)):
+            held_ref[p] = ref[:, 3 * width :]
+        held_ref[3] = corner_ref[:, width:]
+
+
+def project_kernel(one_ref, two_ref, att_ref, y_ref, x_ref, corner_ref, out_ref, held_ref):
+    heads_out(held_ref, (att_ref, y_ref, x_ref, corner_ref))
+    half = att_ref.shape[0]
     one, two = one_ref[...], two_ref[...]
-    out_ref[:, :half] = (nt(one, voa_ref[:, width:]) + nt(two, voc_ref[:, width:])).astype(LOW)
-    out_ref[:, half:] = (nt(one, vob_ref[:, width:]) + nt(two, vod_ref[:, width:])).astype(LOW)
-
-
-def gate_up(hidden, ga_ref, gb_ref, ua_ref, ub_ref, gate_ref, up_ref, act_ref):
-    half = ga_ref.shape[0]
+    out_ref[:, :half] = (nt(one, held_ref[0]) + nt(two, held_ref[2])).astype(LOW)
+    out_ref[:, half:] = (nt(one, held_ref[1]) + nt(two, held_ref[3])).astype(LOW)
+
+
+def blocks(refs, x, y, kind):
+    own_ref, y_ref, x_ref, low_ref, high_ref = refs
+    hid = own_ref.shape[1] // 3
+    if x and y:
+        cut = hid // 2
+        if kind == 0:
+            return [low_ref[:, :hid]]
+        if kind == 1:
+            return [low_ref[:, hid:], high_ref[:, :cut]]
+        return [high_ref[:, cut:]]
+    ref = (x_ref if x else y_ref) if x or y else own_ref
+    return [ref[:, kind * hid : (kind + 1) * hid]]
+
+
+def onto(rows, parts):
+    made = [nn(rows, p) for p in parts]
+    return made[0] if len(made) == 1 else jnp.concatenate(made, axis=1)
+
+
+def back_from(grads, parts):
+    start, total = 0, 0.0
+    for p in parts:
+        total = total + nt(grads[:, start : start + p.shape[1]], p)
+        start += p.shape[1]
+    return total
+
+
+def gate_up(hidden, refs, x, gate_ref, up_ref, act_ref):
+    half = refs[0].shape[0]
     first, second = hidden[:, :half], hidden[:, half:]
-    gate = nn(first, ga_ref[...]) + nn(second, gb_ref[...])
-    up = nn(first, ua_ref[...]) + nn(second, ub_ref[...])
+    gate = onto(first, blocks(refs, x, 0, 0)) + onto(second, blocks(refs, x, 1, 0))
+    up = onto(first, blocks(refs, x, 0, 1)) + onto(second, blocks(refs, x, 1, 1))
     gate_ref[...] = gate
     up_ref[...] = up
     act_ref[...] = (gate * jax.nn.sigmoid(gate) * up).astype(LOW)
 
 
 def enter_kernel(
-    rows_ref, mine_ref, theirs_ref, gain_ref, ga_ref, gb_ref, ua_ref, ub_ref,
+    rows_ref, mine_ref, theirs_ref, gain_ref, own_ref, y_ref,
     normed_ref, inv_ref, hidden_ref, gate_ref, up_ref, act_ref,
 ):
     residual = rows_ref[...].astype(FULL) + add(mine_ref[...], theirs_ref[...])
@@ -328,27 +363,29 @@
     normed_ref[...] = normed
     inv_ref[...] = inv
     hidden_ref[...] = hidden
-    gate_up(hidden, ga_ref, gb_ref, ua_ref, ub_ref, gate_ref, up_ref, act_ref)
-
-
-def more_kernel(hidden_ref, ga_ref, gb_ref, ua_ref, ub_ref, gate_ref, up_ref, act_ref):
-    gate_up(hidden_ref[...], ga_ref, gb_ref, ua_ref, ub_ref, gate_ref, up_ref, act_ref)
-
-
-def down_kernel(one_ref, two_ref, da_ref, db_ref, dc_ref, dd_ref, out_ref):
-    half = da_ref.shape[0]
-    one, two = one_ref[...], two_ref[...]
-    out_ref[:, :half] = (nt(one, da_ref[...]) + nt(two, dc_ref[...])).astype(LOW)
-    out_ref[:, half:] = (nt(one, db_ref[...]) + nt(two, dd_ref[...])).astype(LOW)
+    gate_up(hidden, (own_ref, y_ref, None, None, None), 0, gate_ref, up_ref, act_ref)
+
+
+def rest_kernel(
+    hidden_ref, act1_ref, own_ref, y_ref, x_ref, low_ref, high_ref,
+    gate_ref, up_ref, act_ref, out_ref,
+):
+    refs = (own_ref, y_ref, x_ref, low_ref, high_ref)
+    half = own_ref.shape[0]
+    gate_up(hidden_ref[...], refs, 1, gate_ref, up_ref, act_ref)
+    one, two = act1_ref[...], act_ref[...]
+    for y in range(2):
+        part = back_from(one, blocks(refs, 0, y, 2)) + back_from(two, blocks(refs, 1, y, 2))
+        out_ref[:, y * half : (y + 1) * half] = part.astype(LOW)
 
 
 def back_kernel(
     normed_ref, mine_ref, theirs_ref, up_rows_ref, gate1_ref, up1_ref, gate2_ref, up2_ref,
-    gain1_ref, gain2_ref, da_ref, db_ref, dc_ref, dd_ref,
-    ga_ref, gb_ref, ua_ref, ub_ref, gc_ref, gd_ref, uc_ref, ud_ref,
-    out_ref, grad_ref, low_ref, gg1_ref, ug1_ref, gg2_ref, ug2_ref, mid_ref, sum_ref,
+    gain1_ref, gain2_ref, own_ref, y_ref, x_ref, low_ref, high_ref,
+    out_ref, grad_ref, grad_low_ref, gg_ref, ug_ref, mid_ref, sum_ref,
 ):
-    half = da_ref.shape[0]
+    refs = (own_ref, y_ref, x_ref, low_ref, high_ref)
+    half, hid = own_ref.shape[0], gate1_ref.shape[1]
     residual = normed_ref[...] * gain1_ref[...] + add(mine_ref[...], theirs_ref[...])
     inv = rms_scale(residual)
     normed = residual * inv
@@ -359,36 +396,33 @@
     grad = norm_back(upstream * gain, normed, inv)
     low = grad.astype(LOW)
     grad_ref[...] = grad
-    low_ref[...] = low
+    grad_low_ref[...] = low
     first, second = low[:, :half], low[:, half:]
-
-    def hidden_grads(da_ref, db_ref, gate_ref, up_ref, gg_ref, ug_ref):
-        act_grad = nn(first, da_ref[...]) + nn(second, db_ref[...])
+    grads = []
+    for x, gate_ref, up_ref in ((0, gate1_ref, up1_ref), (1, gate2_ref, up2_ref)):
+        act_grad = onto(first, blocks(refs, x, 0, 2)) + onto(second, blocks(refs, x, 1, 2))
         gate = gate_ref[...]
         sig = jax.nn.sigmoid(gate)
         gg = (act_grad * up_ref[...] * (sig * (1.0 + gate * (1.0 - sig)))).astype(LOW)
         ug = (act_grad * (gate * sig)).astype(LOW)
-        gg_ref[...] = gg
-        ug_ref[...] = ug
-        return gg, ug
-
-    gg1, ug1 = hidden_grads(da_ref, db_ref, gate1_ref, up1_ref, gg1_ref, ug1_ref)
-    gg2, ug2 = hidden_grads(dc_ref, dd_ref, gate2_ref, up2_ref, gg2_ref, ug2_ref)
-    mid_ref[:, :half] = (
-        nt(gg1, ga_ref[...]) + nt(ug1, ua_ref[...]) + nt(gg2, gc_ref[...]) + nt(ug2, uc_ref[...])
-    ).astype(LOW)
-    mid_ref[:, half:] = (
-        nt(gg1, gb_ref[...]) + nt(ug1, ub_ref[...]) + nt(gg2, gd_ref[...]) + nt(ug2, ud_ref[...])
-    ).astype(LOW)
+        gg_ref[:, x * hid : (x + 1) * hid] = gg
+        ug_ref[:, x * hid : (x + 1) * hid] = ug
+        grads.append((gg, ug))
+    for y in range(2):
+        total = 0.0
+        for x in range(2):
+            for kind in range(2):
+                total = total + back_from(grads[x][kind], blocks(refs, x, y, kind))
+        mid_ref[:, y * half : (y + 1) * half] = total.astype(LOW)
 
 
 def leave_kernel(
     grad_two_ref, mine_ref, theirs_ref, normed_ref, inv_ref,
-    gain_ref, voa_ref, vob_ref, voc_ref, vod_ref,
-    grad_ref, low_ref, ctx1_ref, ctx2_ref, sum_ref,
+    gain_ref, att_ref, y_ref, x_ref, corner_ref,
+    grad_ref, low_ref, ctx1_ref, ctx2_ref, sum_ref, held_ref,
 ):
-    half = voa_ref.shape[0]
-    width = ctx1_ref.shape[1]
+    heads_out(held_ref, (att_ref, y_ref, x_ref, corner_ref))
+    half = att_ref.shape[0]
     hidden_grad = grad_two_ref[...] + add(mine_ref[...], theirs_ref[...])
     normed = normed_ref[...]
     column_sum(sum_ref, hidden_grad * normed)
@@ -397,25 +431,25 @@
     grad_ref[...] = grad
     low_ref[...] = low
     first, second = low[:, :half], low[:, half:]
-    ctx1_ref[...] = (nn(first, voa_ref[:, width:]) + nn(second, vob_ref[:, width:])).astype(LOW)
-    ctx2_ref[...] = (nn(first, voc_ref[:, width:]) + nn(second, vod_ref[:, width:])).astype(LOW)
+    ctx1_ref[...] = (nn(first, held_ref[0]) + nn(second, held_ref[1])).astype(LOW)
+    ctx2_ref[...] = (nn(first, held_ref[2]) + nn(second, held_ref[3])).astype(LOW)
 
 
 def input_kernel(
-    qk1_ref, v1_ref, qk2_ref, v2_ref,
-    qka_ref, qkb_ref, qkc_ref, qkd_ref, voa_ref, vob_ref, voc_ref, vod_ref,
+    qk1_ref, v1_ref, qk2_ref, v2_ref, att_ref, y_ref, x_ref, qk_corner_ref, vo_corner_ref,
     full_ref, low_ref,
 ):
-    half = qka_ref.shape[0]
+    half = att_ref.shape[0]
     width = v1_ref.shape[1]
     qk1, v1, qk2, v2 = qk1_ref[...], v1_ref[...], qk2_ref[...], v2_ref[...]
+    pair = 2 * width
     first = (
-        nt(qk1, qka_ref[...]) + nt(v1, voa_ref[:, :width])
-        + nt(qk2, qkc_ref[...]) + nt(v2, voc_ref[:, :width])
+        nt(qk1, att_ref[:, :pair]) + nt(v1, att_ref[:, pair : pair + width])
+        + nt(qk2, x_ref[:, :pair]) + nt(v2, x_ref[:, pair : pair + width])
     )
     second = (
-        nt(qk1, qkb_ref[...]) + nt(v1, vob_ref[:, :width])
-        + nt(qk2, qkd_ref[...]) + nt(v2, vod_ref[:, :width])
+        nt(qk1, y_ref[:, :pair]) + nt(v1, y_ref[:, pair : pair + width])
+        + nt(qk2, qk_corner_ref[...]) + nt(v2, vo_corner_ref[:, :width])
     )
     full_ref[:, :half] = first
     full_ref[:, half:] = second
@@ -466,156 +500,150 @@
     half = D // 2
     hid = down_weight.shape[0]
 
+    bits = wide_bits()
+    near = bits[:-1]
+    half = D // 2
+    hid = down_weight.shape[0]
+    pair = 2 * cols
+
     attend_low = attend_weight.astype(LOW)
     att = jnp.concatenate(
         [attend_low[0], attend_low[1], attend_low[2], output_weight.T.astype(LOW)], axis=1
     )
-    gu = jnp.concatenate([gated_weight[0], gated_weight[1]], axis=1).astype(LOW)
-    down = down_weight.T.astype(LOW)
+    ffn = jnp.concatenate([gated_weight[0], gated_weight[1], down_weight.T], axis=1).astype(LOW)
 
     order = me ^ jnp.array(block_masks(), jnp.int32)
     source = (order[:, None] * block + jnp.arange(block)[None, :]).reshape(1, D)
     mover = (lax.broadcasted_iota(jnp.int32, (D, D), 0) == source).astype(LOW)
 
-    def whole_sequence(own):
-        moved = jnp.dot(own, mover, preferred_element_type=FULL).astype(LOW)
-        received = swap(moved, "narrow", 1)
+    def both_halves(mine, theirs):
         return jnp.where(
             core == 0,
-            jnp.concatenate([moved, received], axis=0),
-            jnp.concatenate([received, moved], axis=0),
+            jnp.concatenate([mine, theirs], axis=0),
+            jnp.concatenate([theirs, mine], axis=0),
         )
 
     def own_rows(value):
         return lax.dynamic_slice_in_dim(value, core * rows, rows, axis=0)
 
     first = widen(att, near[:1])
-    gu = widen(after(gu, first), near[:1])
+    gains = widen(norm_gains.astype(LOW).astype(FULL)[None], bits)
+    moved_in = jnp.dot(layer_input, mover, preferred_element_type=FULL).astype(LOW)
+    moved_up = jnp.dot(layer_cotangent, mover, preferred_element_type=FULL).astype(LOW)
+    other_in = swap(moved_in, "narrow", 1)
+    other_up = swap(moved_up, "narrow", 1)
+    ffn = widen(after(ffn, first), near[:1])
     att = widen(first, near[1:])
+    att, other_in, other_up, gains = lax.optimization_barrier((att, other_in, other_up, gains))
     att_y = swap(att, "wide", 1)
     att_x = swap(att, "narrow", 2)
-    gu = widen(after(gu, att), near[1:])
-    down = widen(after(down, att), near[:1])
-    gains = norm_gains.astype(LOW).astype(FULL)[None]
-    gains = widen(after(gains, att), bits)
+    ffn = widen(after(ffn, att), near[1:])
     gains = gains.transpose(1, 0, 2).reshape(2, 1, D)
-    inputs = whole_sequence(layer_input)
-    upstream = whole_sequence(layer_cotangent)
+    inputs = both_halves(moved_in, other_in)
+    upstream = both_halves(moved_up, other_up)
     cosine, sine = rope_tables()
 
-    inputs, att, att_y, att_x, gu, down, gains, upstream, cosine, sine = lax.optimization_barrier(
-        (inputs, att, att_y, att_x, gu, down, gains, upstream, cosine, sine)
-    )
-    pair = 2 * cols
+    inputs, att, att_y, att_x, ffn, gains, upstream, cosine, sine = lax.optimization_barrier(
+        (inputs, att, att_y, att_x, ffn, gains, upstream, cosine, sine)
+    )
     qk_corner = swap(att_y[:, :pair], "narrow", 2)
     vo_corner = swap(att_x[:, pair:], "wide", 1)
-    gu_y = swap(gu, "wide", 1)
-    gu_x = swap(gu, "narrow", 2)
-    down = widen(down, near[1:])
+    ffn_y = swap(ffn, "wide", 1)
+    ffn_x = swap(ffn, "narrow", 2)
     qk = [[(att, pair, 0), (att_y, pair, 0)], [(att_x, pair, 0), qk_corner]]
     vo = [[(att, pair, 1), (att_y, pair, 1)], [(att_x, pair, 1), vo_corner]]
     saved = [attend_forward(inputs, qk[0], vo[0], cosine, sine)]
-    second_in = after(inputs, saved[0][3], down)
+    second_in = after(inputs, saved[0][3])
     saved.append(attend_forward(second_in, qk[1], vo[1], cosine, sine))
     context = [s[3] for s in saved]
 
-    gu_y, gu_x, context, down = lax.optimization_barrier((gu_y, gu_x, context, down))
-    gate_corner = swap(gu_y[:, :hid], "narrow", 2)
-    up_corner = swap(gu_x[:, hid:], "wide", 1)
-    down_y = swap(down, "wide", 1)
-    down_x = swap(down, "narrow", 2)
-    gate_w = [[(gu, hid, 0), (gu_y, hid, 0)], [(gu_x, hid, 0), gate_corner]]
-    up_w = [[(gu, hid, 1), (gu_y, hid, 1)], [(gu_x, hid, 1), up_corner]]
+    ffn_y, ffn_x, context = lax.optimization_barrier((ffn_y, ffn_x, context))
+    middle = ffn.shape[1] // 2
+    ffn_low = swap(ffn_y[:, :middle], "narrow", 2)
+    ffn_high = swap(ffn_x[:, middle:], "wide", 1)
+    ffn_all = [ffn, ffn_y, ffn_x, ffn_low, ffn_high]
+    att_out = [att, att_y, att_x, vo_corner]
+    held = [pltpu.VMEM((4, half, cols), LOW)]
     (attn_part,) = by_rows(
-        project_kernel, "project", 1.3e9, context, vo[0] + vo[1], [(D, LOW)]
+        project_kernel, "project", 2e9, context, att_out, [(D, LOW)], scratch=held
     )
     attn_other = swap(attn_part, "narrow", 1)
     flow = [(hid, FULL), (hid, FULL), (hid, LOW)]
     normed_one, inv_one, hidden_low, gate1, up1, act1 = by_rows(
-        enter_kernel, "enter", 2e9, [inputs, attn_part, attn_other],
-        [gains[0], *gate_w[0], *up_w[0]], [(D, FULL), (1, FULL), (D, LOW)] + flow,
-    )
-    down_y, down_x, hidden_low = lax.optimization_barrier((down_y, down_x, hidden_low))
-    down_corner = swap(down_y, "narrow", 2)
-    gate2, up2, act2 = by_rows(
-        more_kernel, "more", 2e9, [hidden_low], [*gate_w[1], *up_w[1]], flow
-    )
-    down_w = [down, down_y, down_x, down_corner]
-    (ffn_part,) = by_rows(down_kernel, "down", 2e9, [act1, act2], down_w, [(D, LOW)])
+        enter_kernel, "enter", 4e9, [inputs, attn_part, attn_other],
+        [gains[0], ffn, ffn_y], [(D, FULL), (1, FULL), (D, LOW)] + flow,
+    )
+    gate2, up2, act2, ffn_part = by_rows(
+        rest_kernel, "rest", 5e9, [hidden_low, act1], ffn_all, flow + [(D, LOW)]
+    )
     ffn_other = swap(ffn_part, "narrow", 1)
 
-    (
-        layer_output, grad_two, grad_two_low, gg1, ug1, gg2, ug2, mid_part, gain_two_grad,
-    ) = by_rows(
-        back_kernel, "back", 6e9,
+    layer_output, grad_two, grad_two_low, gg, ug, mid_part, gain_two_grad = by_rows(
+        back_kernel, "back", 9e9,
         [normed_one, ffn_part, ffn_other, upstream, gate1, up1, gate2, up2],
-        [gains[0], gains[1], *down_w, *gate_w[0], *up_w[0], *gate_w[1], *up_w[1]],
-        [(D, LOW), (D, FULL), (D, LOW)] + [(hid, LOW)] * 4 + [(D, LOW)], sums=1,
+        [gains[0], gains[1], *ffn_all],
+        [(D, LOW), (D, FULL), (D, LOW), (2 * hid, LOW), (2 * hid, LOW), (D, LOW)], sums=1,
     )
     mid_other = swap(mid_part, "narrow", 1)
-    ha, hb = hidden_low[:, :half], hidden_low[:, half:]
     down_x = swap(tn(grad_two_low, act2), "narrow", 2)
-    gate_y1 = swap(tn(hb, gg1), "wide", 1)
-    gate_y2 = swap(tn(hb, gg2), "wide", 1)
-    up_x = swap(tn(hidden_low, ug2), "narrow", 2)
+    gate_y = swap(tn(hidden_low[:, half:], gg), "wide", 1)
+    up_send = tn(hidden_low, ug[:, hid:])
     down_own = tn(grad_two_low, act1)
-    gate_1, gate_2 = tn(ha, gg1), tn(ha, gg2)
-    up_own = tn(hidden_low, ug1)
-    mid_part, mid_other, down_own, gate_1, gate_2, up_own = lax.optimization_barrier(
-        (mid_part, mid_other, down_own, gate_1, gate_2, up_own)
+    gate_own = tn(hidden_low[:, :half], gg)
+    mid_part, mid_other, down_own, gate_own, up_send = lax.optimization_barrier(
+        (mid_part, mid_other, down_own, gate_own, up_send)
     )
     grad_one, grad_one_low, dctx1, dctx2, gain_one_grad = by_rows(
-        leave_kernel, "leave", 2e9, [grad_two, mid_part, mid_other, normed_one, inv_one],
-        [gains[0], *vo[0], *vo[1]],
-        [(D, FULL), (D, LOW), (context[0].shape[1], LOW), (context[0].shape[1], LOW)], sums=1,
-    )
+        leave_kernel, "leave", 4e9, [grad_two, mid_part, mid_other, normed_one, inv_one],
+        [gains[0], *att_out], [(D, FULL), (D, LOW), (cols, LOW), (cols, LOW)], sums=1, scratch=held,
+    )
+
+    down_x, gate_y, up_send, grad_one_low = lax.optimization_barrier(
+        (down_x, gate_y, up_send, grad_one_low)
+    )
+    up_x = swap(up_send, "narrow", 2)
+    down_sum, gate_sum = add(down_own, down_x), add(gate_own, gate_y)
+    down_far, gate_far = down_sum[half:].astype(LOW), gate_sum[:, hid:].astype(LOW)
+    down_y = swap(down_far, "wide", 1)
+    gate_x = swap(gate_far, "narrow", 2)
 
     q, k, v, _, lse = saved[1]
-    dqk2, dv2 = attend_backward(q, k, v, lse, dctx2, cosine, sine)
+    dqk2, dv2 = attend_backward(q, k, v, lse, after(dctx2, down_far, gate_far), cosine, sine)
     xa, xb = inputs[:, :half], inputs[:, half:]
-    d_out2 = tn(grad_one_low, context[1])
-    vo2 = jnp.concatenate([tn(inputs, dv2), d_out2], axis=1)
-    vo_x = swap(vo2, "narrow", 2)
-    qk_y2 = swap(tn(xb, dqk2), "wide", 1)
-    qk_2 = tn(xa, dqk2)
-    down_sum = add(down_own, down_x)
-    gate_sum1, gate_sum2 = add(gate_1, gate_y1), add(gate_2, gate_y2)
-    dctx1, down_sum, gate_sum1, gate_sum2, qk_2 = lax.optimization_barrier(
-        (dctx1, down_sum, gate_sum1, gate_sum2, qk_2)
-    )
-    down_y = swap(down_sum[half:].astype(LOW), "wide", 1)
-    gate_x = swap(gate_sum2.astype(LOW), "narrow", 2)
+    vo_send = jnp.concatenate([tn(inputs, dv2), tn(grad_one_low, context[1])], axis=1)
+    vo_x = swap(vo_send, "narrow", 2)
+    qk_send2 = tn(xb, dqk2)
+    qk_y2 = swap(qk_send2, "wide", 1)
+    back = near[::-1]
+    early = jnp.concatenate([add(down_sum[:half], down_y), add(gate_sum[:, :hid], gate_x)], axis=1)
     q, k, v, _, lse = saved[0]
-    dqk1, dv1 = attend_backward(q, k, v, lse, dctx1, cosine, sine)
-    qk_y1 = swap(tn(xb, dqk1), "wide", 1)
-    vo1 = jnp.concatenate([tn(inputs, dv1), tn(grad_one_low, context[0])], axis=1)
-    qk_1 = tn(xa, dqk1)
-
-    up_sum = add(up_own, up_x)
-    up_y = swap(up_sum[half:].astype(LOW), "wide", 1)
-    back = near[::-1]
-    down_red = narrow_down(add(down_sum[:half], down_y), back)
-    gate_red = narrow_down(add(gate_sum1, gate_x), back)
-    vo_sum = add(vo1, vo_x)
-    vo_y = swap(vo_sum[half:].astype(LOW), "wide", 1)
-    qk_sum = add(qk_1, qk_y1)
-    qk_x = swap(add(qk_2, qk_y2).astype(LOW), "narrow", 2)
+    dctx1, early, up_x = lax.optimization_barrier(
+        (after(dctx1, vo_send, qk_send2), early, up_x)
+    )
+    up_sum = add(tn(hidden_low, ug[:, :hid]), up_x)
+    up_far = up_sum[half:].astype(LOW)
+    up_y = swap(up_far, "wide", 1)
+    early_red = narrow_down(early, back)
+    dqk1, dv1 = attend_backward(q, k, v, lse, after(dctx1, up_far), cosine, sine)
+    qk_send1 = tn(xb, dqk1)
+    qk_y1 = swap(qk_send1, "wide", 1)
+    dqk1, dv1, qk_send1 = lax.optimization_barrier((dqk1, dv1, qk_send1))
+    vo_sum = add(
+        jnp.concatenate([tn(inputs, dv1), tn(grad_one_low, context[0])], axis=1), vo_x
+    )
+    vo_far = vo_sum[half:].astype(LOW)
+    vo_y = swap(vo_far, "wide", 1)
+    qk_far = add(tn(xa, dqk2), qk_y2).astype(LOW)
+    qk_x = swap(qk_far, "narrow", 2)
+    qk_sum = add(tn(xa, dqk1), qk_y1)
+    part_full, part_low = by_rows(
+        input_kernel, "inputs", 4e9, [after(dqk1, vo_far, qk_far), dv1, dqk2, dv2],
+        [att, att_y, att_x, qk_corner, vo_corner], [(D, FULL), (D, LOW)],
+    )
     up_red = narrow_down(add(up_sum[:half], up_y), back)
     last = jnp.concatenate([add(qk_sum, qk_x), add(vo_sum[:half], vo_y)], axis=1)
     att_red = narrow_down(last, back)
 
-    gain_red = jnp.concatenate([gain_one_grad, gain_two_grad], axis=0).reshape(2, wide, block)
-    gain_red = gain_red.transpose(1, 0, 2)
-    gain_red = gain_red + swap(gain_red, "narrow", 2)
-    for bit in bits[::-1]:
-        part = gain_red.shape[0] // 2
-        gain_red = gain_red[:part] + swap(gain_red[part:], "wide", bit)
-    gain_red = gain_red[0]
-
-    part_full, part_low = by_rows(
-        input_kernel, "inputs", 2e9, [dqk1, dv1, dqk2, dv2],
-        qk[0] + qk[1] + vo[0] + vo[1], [(D, FULL), (D, LOW)],
-    )
     theirs = lax.dynamic_slice_in_dim(part_low, (1 - core) * rows, rows, axis=0)
     input_grad = own_rows(grad_one) + own_rows(part_full) + swap(theirs, "narrow", 1).astype(FULL)
     input_grad = lax.dot_general(
@@ -624,17 +652,29 @@
     )
     layer_output = nt(own_rows(layer_output), mover).astype(LOW)
 
-    square = sum(jnp.sum(g * g) for g in (att_red, gate_red, up_red, down_red))
-    square = square + jnp.where(narrow == 0, jnp.sum(gain_red * gain_red), 0.0)
-    total = tree_sum(jnp.full((1, 128), square, FULL), "narrow")
-    total = tree_sum(total, "wide")[0, 0]
+    gain_grads = lax.dot_general(
+        jnp.concatenate([gain_one_grad, gain_two_grad], axis=0), mover.astype(FULL),
+        (((1,), (1,)), ((), ())), precision=lax.Precision.HIGHEST, preferred_element_type=FULL,
+    )
+
+    square = jnp.sum(early_red * early_red) + jnp.sum(up_red * up_red)
+    square = jnp.full((1, 128), square + jnp.sum(att_red * att_red), FULL)
+    square = square + swap(square, "narrow", 1)
+    message = jnp.concatenate([gain_grads.reshape(1, 2 * D), square], axis=1)
+    message = message + swap(message, "narrow", 2)
+    for bit in bits[::-1]:
+        message = message + swap(message, "wide", bit)
+    gain_sum = message[:, : 2 * D]
+    total = message[0, 2 * D] + jnp.sum(gain_sum * gain_sum)
+    gain_red = lax.dynamic_index_in_dim(gain_sum.reshape(2, wide, block), me, 1, keepdims=False)
     grad_norm = jnp.sqrt(total)
     all_tokens = rows * wide * lax.axis_size("narrow")
     clip = 0.02 * math.sqrt(all_tokens * (4 * D * D + 3 * D * FF + 2 * D))
     ratio = clip / jnp.maximum(grad_norm, clip)
     attend_red = jnp.stack([att_red[:, k * cols : (k + 1) * cols] for k in range(3)])
     output_red = att_red[:, 3 * cols :].T
-    gated_red = jnp.stack([gate_red, up_red])
+    down_red = early_red[:, :hid].T
+    gated_red = jnp.stack([early_red[:, hid:], up_red])
     new_attend = adam_update(
         attend_weight, attend_first, attend_second, attend_red, ratio, D ** (-0.5), WEIGHT_DECAY
     )
@@ -646,7 +686,7 @@
         gated_weight, gated_first, gated_second, gated_red, ratio, D ** (-0.5), WEIGHT_DECAY
     )
     new_down = adam_update(
-        down_weight, down_first, down_second, down_red.T, ratio, FF ** (-0.5), WEIGHT_DECAY
+        down_weight, down_first, down_second, down_red, ratio, FF ** (-0.5), WEIGHT_DECAY
     )
     new_gains = adam_update(norm_gains, gains_first, gains_second, gain_red, ratio, 0.4, 0.0)
     return (

time: 323 us -> 328 us (1.015)
  waiting for transfers between devices: 83.8 us -> 104 us
  local copies, waits for them, and re-layouts: 26.2 us -> 42.7 us
  matrix products: 32.3 us -> 20.5 us
  other arithmetic: 32.8 us -> 24.1 us
  Pallas kernels: 84.5 us -> 76.4 us
    ppermute x55 -> x43, waiting for transfers between devices: 83.8 us -> 104 us  [swap(): return lax.ppermute(value, axis, [(i, i ^ bit) for i in range(size)])]
    unnamed x204 -> x188, local copies, waits for them, and re-layouts: 19.8 us -> 37.7 us
    dot_general x16 -> x14, matrix products: 22.4 us -> 10.7 us  [tn(): lax.dot_general(rows, grads, (((0,), (0,)), ((), ())), preferred_element_...]
    add x13 -> x11, other arithmetic: 11.7 us -> 1.48 us  [add(): return kept.astype(FULL) + received.astype(FULL)]
    pallas_call x7 -> x6, Pallas kernels: 45.5 us -> 37.3 us  [by_rows(): pl.pallas_call(kernel, grid=(L // QB,), in_specs=specs + [held_once(f) fo...]
    ppermute x55 -> x43, starting transfers between devices: 52.8 us -> 49.9 us  [swap(): return lax.ppermute(value, axis, [(i, i ^ bit) for i in range(size)])]
  transfers between devices with their start and end apart: 55 -> 43, of which waited for: 22 -> 21; matrix products, arithmetic and copies ran while one was open for 21% -> 15% of each run, Pallas kernels for 20% -> 17%
where the time goes in v1:
time: 328 us; the launch traced here: 324 us
  waiting for transfers between devices  104 us (32%)
  Pallas kernels  76.4 us (23%)
  starting transfers between devices  49.9 us (15%)
  local copies, waits for them, and re-layouts  42.7 us (13%)
  other arithmetic  24.1 us (7%)
  matrix products  20.5 us (6%)
  between operations  6.67 us (2%)
    ppermute x43, waiting for transfers between devices, swap(): return lax.ppermute(value, axis, [(i, i ^ bit) for i in range(size)])  104 us
    ppermute x43, starting transfers between devices, swap(): return lax.ppermute(value, axis, [(i, i ^ bit) for i in range(size)])  49.9 us
    unnamed x188, local copies, waits for them, and re-layouts  37.7 us
    pallas_call x6, Pallas kernels, by_rows(): pl.pallas_call(kernel, grid=(L // QB,), in_specs=specs + [held_once(f) fo...  37.3 us
    pallas_call x2, Pallas kernels, attend_forward(): pl.pallas_call(attend_kernel, grid=(1,), in_specs=list(specs), out_specs=...  19.7 us
    pallas_call x2, Pallas kernels, attend_backward(): pl.pallas_call(attend_back_kernel, out_shape=(jax.ShapeDtypeStruct((L, 2...  19.4 us
    dot_general x14, matrix products, tn(): lax.dot_general(rows, grads, (((0,), (0,)), ((), ())), preferred_element_...  10.7 us
  transfers between devices with their start and end apart: 43, of which 21 were waited for; matrix products, arithmetic and copies ran while one was open for 15% of the time, Pallas kernels for 17%

profile of v1, /device:TPU:0, one launch (start us, length us, event | category | flops | bytes accessed | tf_op | source)
XLA Modules:
  0.0 324.0 jit_solution(15731560307707932621)
XLA Ops:
  2.8 4.1 %collective-permute-start = (bf16[96,768]{1,0:T(8,128)(2,1)S(1)}, bf16[96,768]{1,0:T(8,128)(2,1)S(1)}, u32[]{:S(2)}, u32[]{:S(2)}) collective-permute-start(bf16[96,768]{1,0:T(8,128)(2,1)S(1)} %pad_maximum_fusion.8), channel_id=1, source_target_pairs={{0,16},{4,20},{8,24},{12,28},{16,0},{20,4},{24,8},{28,12},{1,17},{... | collective-permute-start | bytes 442376 | tf_op jit(solution)/shard_map/ppermute | solution.py:29
  22.2 7.8 %collective-permute-done.1 = bf16[192,768]{1,0:T(8,128)(2,1)S(1)} collective-permute-done((bf16[192,768]{1,0:T(8,128)(2,1)S(1)}, bf16[192,768]{1,0:T(8,128)(2,1)S(1)}, u32[]{:S(2)}, u32[]{:S(2)}) %collective-permute-start.1) | collective-permute-done | bytes 294944 | tf_op jit(solution)/shard_map/ppermute | solution.py:29
  40.3 4.1 %maximum_select_fusion = (bf16[1024,768]{1,0:T(8,128)(2,1)S(1)}, bf16[1024,768]{1,0:T(8,128)(2,1)}) fusion(bf16[512,768]{1,0:T(8,128)(2,1)} %copy-done.74, bf16[512,768]{1,0:T(8,128)(2,1)} %copy-done.73, pred[]{:T(512)S(6)} %eq.17, bf16[512,768]{1,0:T(8,128)(2,1)} %copy-done.75, bf16[512,768]{1,0:T(8,128)(2,1)} %copy-done.76), kind=kLoop, calls=%fused_computation.6 | loop fusion | flops 14155776 | bytes 6291457 | tf_op jit(solution)/shard_map/jit(_where)/select_n | solution.py:520
  55.6 9.8 %attend_forward.2 = (bf16[3,1024,64]{2,1,0:T(8,128)(2,1)S(1)}, bf16[3,1024,64]{2,1,0:T(8,128)(2,1)S(1)}, bf16[3,1024,64]{2,1,0:T(8,128)(2,1)S(1)}, bf16[1024,192]{1,0:T(8,128)(2,1)S(1)}, f32[3,1,1024]{2,1,0:T(1,128)S(1)}) custom-call(bf16[1024,768]{1,0:T(8,128)(2,1)S(1)} %get-tuple-element.107.rows_ref, ...), custom_call_target="tpu_custom_call" | custom-call | flops 8000000000 | bytes 8388608 | tf_op jit(solution)/shard_map/attend_forward/pallas_call | solution.py:170
  66.3 15.7 %collective-permute-done.13.qkb_ref.qk_corner_ref = bf16[384,384]{1,0:T(8,128)(2,1)S(1)} collective-permute-done((bf16[384,384]{1,0:T(8,128)(2,1)S(1)}, bf16[384,384]{1,0:T(8,128)(2,1)S(1)}, u32[]{:S(2)}, u32[]{:S(2)}) %collective-permute-start.13) | collective-permute-done | bytes 294944 | tf_op jit(solution)/shard_map/ppermute | solution.py:29
  82.0 9.9 %attend_forward.3 = (bf16[3,1024,64]{2,1,0:T(8,128)(2,1)S(1)}, bf16[3,1024,64]{2,1,0:T(8,128)(2,1)S(1)}, bf16[3,1024,64]{2,1,0:T(8,128)(2,1)S(1)}, bf16[1024,192]{1,0:T(8,128)(2,1)S(1)}, f32[3,1,1024]{2,1,0:T(1,128)S(1)}) custom-call(bf16[1024,768]{1,0:T(8,128)(2,1)S(1)} %get-tuple-element.107.rows_ref, ...), custom_call_target="tpu_custom_call" | custom-call | flops 8000000000 | bytes 8388608 | tf_op jit(solution)/shard_map/attend_forward/pallas_call | solution.py:170
  94.8 4.3 %project.1.mine_ref = bf16[1024,768]{1,0:T(8,128)(2,1)S(1)} custom-call(bf16[1024,192]{1,0:T(8,128)(2,1)S(1)} %get-tuple-element.110.one_ref, bf16[1024,192]{1,0:T(8,128)(2,1)S(1)} %get-tuple-element.111.two_ref, bf16[384,768]{1,0:T(8,128)(2,1)S(1)} %pad_maximum_fusion.3.qka_ref.voa_ref.att_ref, ...), custom_call_target="tpu_custom_call" | custom-call | flops 2000000000 | bytes 16777216 | tf_op jit(solution)/shard_map/project/pallas_call | solution.py:268
  102.5 3.8 %enter.1 = (f32[1024,768]{1,0:T(8,128)S(1)}, f32[1024,1]{1,0:T(8,128)S(1)}, bf16[1024,768]{1,0:T(8,128)(2,1)S(1)}, f32[1024,512]{1,0:T(8,128)S(1)}, f32[1024,512...) custom-call(bf16[1024,768]{1,0:T(8,128)(2,1)S(1)} %get-tuple-element.107.rows_ref, bf16[1024,768]{1,0:T(8,128)(2,1)S(1)} %project.1.mine_ref, ...), custom_call_target="tpu_custom_call" | custom-call | flops 4000000000 | bytes 16777216 | tf_op jit(solution)/shard_map/enter/pallas_call | solution.py:268
  109.4 5.6 %collective-permute-done.16.low_ref = bf16[384,768]{1,0:T(8,128)(2,1)S(1)} collective-permute-done((bf16[384,768]{1,0:T(8,128)(2,1)S(1)}, bf16[384,768]{1,0:T(8,128)(2,1)S(1)}, u32[]{:S(2)}, u32[]{:S(2)}) %collective-permute-start.16) | collective-permute-done | bytes 589856 | tf_op jit(solution)/shard_map/ppermute | solution.py:29
  116.3 6.2 %rest.1 = (f32[1024,512]{1,0:T(8,128)S(1)}, f32[1024,512]{1,0:T(8,128)S(1)}, bf16[1024,512]{1,0:T(8,128)(2,1)S(1)}, bf16[1024,768]{1,0:T(8,128)(2,1)}) custom-call(bf16[1024,768]{1,0:T(8,128)(2,1)S(1)} %get-tuple-element.115.hidden_ref, bf16[1024,512]{1,0:T(8,128)(2,1)S(1)} %get-tuple-element.116.act1_ref, bf16[384,1536]{1,0:T(8,128)(2,1)S(1)} %pad_maximum_fusion.1.own_ref, ...), custom_call_target="tpu_custom_call" | custom-call | flops 5000000000 | bytes 16777216 | tf_op jit(solution)/shard_map/rest/pallas_call | solution.py:268
  143.9 12.2 %back.1 = (bf16[1024,768]{1,0:T(8,128)(2,1)S(1)}, f32[1024,768]{1,0:T(8,128)}, bf16[1024,768]{1,0:T(8,128)(2,1)S(1)}, bf16[1024,1024]{1,0:T(8,128)(2,1)S(1)}, bf...) custom-call(f32[1024,768]{1,0:T(8,128)} %copy-done.38, ...), custom_call_target="tpu_custom_call" | custom-call | flops 8999999488 | bytes 16777216 | tf_op jit(solution)/shard_map/back/pallas_call | solution.py:268
  166.6 5.7 %leave.1 = (f32[1024,768]{1,0:T(8,128)S(1)}, bf16[1024,768]{1,0:T(8,128)(2,1)S(1)}, bf16[1024,192]{1,0:T(8,128)(2,1)S(1)}, bf16[1024,192]{1,0:T(8,128)(2,1)S(1)}, f32[1,768]{1,0:T(1,128)S(1)}) custom-call(f32[1024,768]{1,0:T(8,128)S(1)} %copy-done.40, bf16[1024,768]{1,0:T(8,128)(2,1)S(1)} %get-tuple-element.130.mine_ref, ...), custom_call_target="tpu_custom_call" | custom-call | flops 4000000000 | bytes 16777216 | tf_op jit(solution)/shard_map/leave/pallas_call | solution.py:268
  172.3 4.9 %collective-permute-done.21 = bf16[384,1024]{1,0:T(8,128)(2,1)S(1)} collective-permute-done((bf16[384,1024]{1,0:T(8,128)(2,1)S(1)}, bf16[384,1024]{1,0:T(8,128)(2,1)S(1)}, u32[]{:S(2)}, u32[]{:S(2)}) %collective-permute-start.21) | collective-permute-done | bytes 786464 | tf_op jit(solution)/shard_map/ppermute | solution.py:29
  183.0 9.9 %attend_backward.2 = (bf16[1024,384]{1,0:T(8,128)(2,1)S(1)}, bf16[1024,192]{1,0:T(8,128)(2,1)S(1)}) custom-call(bf16[3,1024,64]{2,1,0:T(8,128)(2,1)S(1)} %copy-done.61, bf16[3,1024,64]{2,1,0:T(8,128)(2,1)S(1)} %copy-done.63, bf16[3,1024,64]{2,1,0:T(8,128)(2,1)S(1)} %copy-done.65, f32[3,1,1024]{2,1,0:T(1,128)S(1)} %get-tuple-element.142.lse_ref, ...), custom_call_target="tpu_custom_call" | custom-call | flops 8999999488 | bytes 8388608 | tf_op jit(solution)/shard_map/attend_backward/pallas_call | solution.py:238
  197.1 3.9 %collective-permute-done.26 = bf16[384,384]{0,1:T(8,128)(2,1)S(1)} collective-permute-done((bf16[384,384]{0,1:T(8,128)(2,1)S(1)}, bf16[384,384]{0,1:T(8,128)(2,1)S(1)}, u32[]{:S(2)}, u32[]{:S(2)}) %collective-permute-start.26) | collective-permute-done | bytes 294944 | tf_op jit(solution)/shard_map/ppermute | solution.py:29
  203.5 24.7 %collective-permute-done.24 = bf16[768,512]{1,0:T(8,128)(2,1)S(1)} collective-permute-done((bf16[768,512]{1,0:T(8,128)(2,1)S(1)}, bf16[768,512]{1,0:T(8,128)(2,1)S(1)}, u32[]{:S(2)}, u32[]{:S(2)}) %collective-permute-start.24) | collective-permute-done | bytes 786464 | tf_op jit(solution)/shard_map/ppermute | solution.py:29
  228.5 9.5 %attend_backward.3 = (bf16[1024,384]{1,0:T(8,128)(2,1)S(1)}, bf16[1024,192]{1,0:T(8,128)(2,1)S(1)}) custom-call(bf16[3,1024,64]{2,1,0:T(8,128)(2,1)S(1)} %copy-done.55, bf16[3,1024,64]{2,1,0:T(8,128)(2,1)S(1)} %copy-done.57, bf16[3,1024,64]{2,1,0:T(8,128)(2,1)S(1)} %copy-done.59, f32[3,1,1024]{2,1,0:T(1,128)S(1)} %get-tuple-element.137.lse_ref, ...), custom_call_target="tpu_custom_call" | custom-call | flops 8999999488 | bytes 8388608 | tf_op jit(solution)/shard_map/attend_backward/pallas_call | solution.py:238
  249.2 4.3 %collective-permute-done.35 = bf16[384,384]{0,1:T(8,128)(2,1)S(1)} collective-permute-done((bf16[384,384]{0,1:T(8,128)(2,1)S(1)}, bf16[384,384]{0,1:T(8,128)(2,1)S(1)}, u32[]{:S(2)}, u32[]{:S(2)}) %collective-permute-start.35) | collective-permute-done | bytes 294944 | tf_op jit(solution)/shard_map/ppermute | solution.py:29
  262.7 3.3 %collective-permute-done.36 = bf16[192,768]{0,1:T(8,128)(2,1)S(1)} collective-permute-done((bf16[192,768]{0,1:T(8,128)(2,1)S(1)}, bf16[192,768]{0,1:T(8,128)(2,1)S(1)}, u32[]{:S(2)}, u32[]{:S(2)}) %collective-permute-start.36) | collective-permute-done | bytes 294944 | tf_op jit(solution)/shard_map/ppermute | solution.py:29
  273.2 6.6 %collective-permute-done.32 = bf16[96,512]{1,0:T(8,128)(2,1)S(1)} collective-permute-done((bf16[96,512]{1,0:T(8,128)(2,1)S(1)}, bf16[96,512]{1,0:T(8,128)(2,1)S(1)}, u32[]{:S(2)}, u32[]{:S(2)}) %collective-permute-start.32) | collective-permute-done | bytes 98336 | tf_op jit(solution)/shard_map/ppermute | solution.py:29
  288.1 5.2 %inputs.1 = (f32[1024,768]{1,0:T(8,128)S(1)}, bf16[1024,768]{1,0:T(8,128)(2,1)S(1)}) custom-call(bf16[1024,384]{1,0:T(8,128)(2,1)S(1)} %copy-done.27, bf16[1024,192]{1,0:T(8,128)(2,1)S(1)} %copy-done.33, bf16[1024,384]{1,0:T(8,128)(2,1)S(1)} %copy-done.37, bf16[1024,192]{1,0:T(8,128)(2,1)S(1)} %copy-done.29, bf16[384,768]{1,0:T(8,128)(2,1)S(1)} %copy-done.10, ...), custom_call_target="tpu_custom_call" | custom-call | flops 4000000000 | bytes 16777216 | tf_op jit(solution)/shard_map/inputs/pallas_call | solution.py:268
  298.8 3.6 %collective-permute-done.41 = f32[1,1664]{1,0:T(1,128)S(1)} collective-permute-done((f32[1,1664]{1,0:T(1,128)S(1)}, f32[1,1664]{1,0:T(1,128)S(1)}, u32[]{:S(2)}, u32[]{:S(2)}) %collective-permute-start.41) | collective-permute-done | bytes 6688 | tf_op jit(solution)/shard_map/ppermute | solution.py:29
  303.5 3.5 %collective-permute-done.42 = f32[1,1664]{1,0:T(1,128)S(1)} collective-permute-done((f32[1,1664]{1,0:T(1,128)S(1)}, f32[1,1664]{1,0:T(1,128)S(1)}, u32[]{:S(2)}, u32[]{:S(2)}) %collective-permute-start.42) | collective-permute-done | bytes 6688 | tf_op jit(solution)/shard_map/ppermute | solution.py:29
  317.4 5.3 %fusion.1 = f32[512,768]{1,0:T(8,128)} fusion(bf16[512,768]{1,0:T(8,128)(2,1)} %collective-permute-done.27, f32[1024,768]{1,0:T(8,128)} %copy-done.7, s32[]{:T(128)S(6)} %select_n.71, f32[1024,768]{1,0:T(8,128)S(1)} %copy-done.6, s32[768]{0:T(1024)S(1)} %add.221), kind=kOutput, calls=%fused_computation.2 | convolution fusion | flops 3625648128 | bytes 5509124 | tf_op jit(solution)/shard_map/dot_general | solution.py:649
  (352 shorter events, 143.6 us)
Async XLA Ops:
  9.4 21.7 %collective-permute-start.2 = (bf16[512,768]{1,0:T(8,128)(2,1)S(1)}, bf16[512,768]{1,0:T(8,128)(2,1)S(1)}, u32[]{:S(2)}, u32[]{:S(2)}) collective-permute-start(bf16[512,768]{1,0:T(8,128)(2,1)S(1)} %fusion.14), channel_id=1, source_target_pairs={{0,1},{1,0},{2,3},{3,2},{4,5},{5,4},{6,7},{7,6},{8,9},{9,8},{10,11... | collective-permute-start | bytes 2359304 | tf_op jit(solution)/shard_map/ppermute | solution.py:29
  10.5 20.5 %collective-permute-start.3 = (bf16[512,768]{1,0:T(8,128)(2,1)S(1)}, bf16[512,768]{1,0:T(8,128)(2,1)S(1)}, u32[]{:S(2)}, u32[]{:S(2)}) collective-permute-start(bf16[512,768]{1,0:T(8,128)(2,1)S(1)} %fusion.13), channel_id=1, source_target_pairs={{0,1},{1,0},{2,3},{3,2},{4,5},{5,4},{6,7},{7,6},{8,9},{9,8},{10,11... | collective-permute-start | bytes 2359304 | tf_op jit(solution)/shard_map/ppermute | solution.py:29
  14.9 15.0 %collective-permute-start.1 = (bf16[192,768]{1,0:T(8,128)(2,1)S(1)}, bf16[192,768]{1,0:T(8,128)(2,1)S(1)}, u32[]{:S(2)}, u32[]{:S(2)}) collective-permute-start(bf16[192,768]{1,0:T(8,128)(2,1)S(1)} %pad_maximum_fusion.6), channel_id=1, source_target_pairs={{0,8},{4,12},{8,0},{12,4},{16,24},{20,28},{24,16},{28,20},{1,9},{5... | collective-permute-start | bytes 884744 | tf_op jit(solution)/shard_map/ppermute | solution.py:29
  16.3 13.8 %collective-permute-start.9 = (bf16[96,1536]{1,0:T(8,128)(2,1)S(1)}, bf16[96,1536]{1,0:T(8,128)(2,1)S(1)}, u32[]{:S(2)}, u32[]{:S(2)}) collective-permute-start(bf16[96,1536]{1,0:T(8,128)(2,1)S(1)} %pad_maximum_fusion.7), channel_id=1, source_target_pairs={{0,16},{4,20},{8,24},{12,28},{16,0},{20,4},{24,8},{28,12},{1,17},{... | collective-permute-start | bytes 884744 | tf_op jit(solution)/shard_map/ppermute | solution.py:29
  31.1 15.8 %collective-permute-start.10 = (bf16[192,1536]{1,0:T(8,128)(2,1)}, bf16[192,1536]{1,0:T(8,128)(2,1)}, u32[]{:S(2)}, u32[]{:S(2)}) collective-permute-start(bf16[192,1536]{1,0:T(8,128)(2,1)} %pad_maximum_fusion.4), channel_id=1, source_target_pairs={{0,8},{4,12},{8,0},{12,4},{16,24},{20,28},{24,16},{28,20},{1,9},{5... | collective-permute-start | bytes 1769480 | tf_op jit(solution)/shard_map/ppermute | solution.py:29
  34.3 14.0 %collective-permute-start.7 = (bf16[384,768]{1,0:T(8,128)(2,1)S(1)}, bf16[384,768]{1,0:T(8,128)(2,1)}, u32[]{:S(2)}, u32[]{:S(2)}) collective-permute-start(bf16[384,768]{1,0:T(8,128)(2,1)S(1)} %pad_maximum_fusion.3.qka_ref.voa_ref.att_ref), channel_id=1, source_target_pairs={{0,4},{4,0},{8,12},{12,8},{16,20},{20,16},{24,28},{28,24},{1,5},{5... | collective-permute-start | bytes 1769480 | tf_op jit(solution)/shard_map/ppermute | solution.py:29
  35.8 13.6 %collective-permute-start.8 = (bf16[384,768]{1,0:T(8,128)(2,1)S(1)}, bf16[384,768]{1,0:T(8,128)(2,1)}, u32[]{:S(2)}, u32[]{:S(2)}) collective-permute-start(bf16[384,768]{1,0:T(8,128)(2,1)S(1)} %pad_maximum_fusion.3.qka_ref.voa_ref.att_ref), channel_id=1, source_target_pairs={{0,2},{1,3},{2,0},{3,1},{4,6},{5,7},{6,4},{7,5},{8,10},{9,11},{10,... | collective-permute-start | bytes 1769480 | tf_op jit(solution)/shard_map/ppermute | solution.py:29
  49.4 45.3 %collective-permute-start.11 = (bf16[384,1536]{1,0:T(8,128)(2,1)S(1)}, bf16[384,1536]{1,0:T(8,128)(2,1)S(1)}, u32[]{:S(2)}, u32[]{:S(2)}) collective-permute-start(bf16[384,1536]{1,0:T(8,128)(2,1)S(1)} %pad_maximum_fusion.1.own_ref), channel_id=1, source_target_pairs={{0,4},{4,0},{8,12},{12,8},{16,20},{20,16},{24,28},{28,24},{1,5},{5... | collective-permute-start | bytes 3538952 | tf_op jit(solution)/shard_map/ppermute | solution.py:29
  49.9 44.8 %collective-permute-start.12 = (bf16[384,1536]{1,0:T(8,128)(2,1)S(1)}, bf16[384,1536]{1,0:T(8,128)(2,1)S(1)}, u32[]{:S(2)}, u32[]{:S(2)}) collective-permute-start(bf16[384,1536]{1,0:T(8,128)(2,1)S(1)} %pad_maximum_fusion.1.own_ref), channel_id=1, source_target_pairs={{0,2},{1,3},{2,0},{3,1},{4,6},{5,7},{6,4},{7,5},{8,10},{9,11},{10,... | collective-permute-start | bytes 3538952 | tf_op jit(solution)/shard_map/ppermute | solution.py:29
  52.4 29.6 %collective-permute-start.13 = (bf16[384,384]{1,0:T(8,128)(2,1)S(1)}, bf16[384,384]{1,0:T(8,128)(2,1)S(1)}, u32[]{:S(2)}, u32[]{:S(2)}) collective-permute-start(bf16[384,384]{1,0:T(8,128)(2,1)S(1)} %slice.154), channel_id=1, source_target_pairs={{0,2},{1,3},{2,0},{3,1},{4,6},{5,7},{6,4},{7,5},{8,10},{9,11},{10,... | collective-permute-start | bytes 884744 | tf_op jit(solution)/shard_map/ppermute | solution.py:29
  54.0 28.0 %collective-permute-start.14 = (bf16[384,384]{1,0:T(8,128)(2,1)S(1)}, bf16[384,384]{1,0:T(8,128)(2,1)S(1)}, u32[]{:S(2)}, u32[]{:S(2)}) collective-permute-start(bf16[384,384]{1,0:T(8,128)(2,1)S(1)} %slice.155), channel_id=1, source_target_pairs={{0,4},{4,0},{8,12},{12,8},{16,20},{20,16},{24,28},{28,24},{1,5},{5... | collective-permute-start | bytes 884744 | tf_op jit(solution)/shard_map/ppermute | solution.py:29
  99.2 15.8 %collective-permute-start.16 = (bf16[384,768]{1,0:T(8,128)(2,1)S(1)}, bf16[384,768]{1,0:T(8,128)(2,1)S(1)}, u32[]{:S(2)}, u32[]{:S(2)}) collective-permute-start(bf16[384,768]{1,0:T(8,128)(2,1)S(1)} %slice.157), channel_id=1, source_target_pairs={{0,2},{1,3},{2,0},{3,1},{4,6},{5,7},{6,4},{7,5},{8,10},{9,11},{10,... | collective-permute-start | bytes 1769480 | tf_op jit(solution)/shard_map/ppermute | solution.py:29
  100.8 15.5 %collective-permute-start.17 = (bf16[384,768]{1,0:T(8,128)(2,1)S(1)}, bf16[384,768]{1,0:T(8,128)(2,1)S(1)}, u32[]{:S(2)}, u32[]{:S(2)}) collective-permute-start(bf16[384,768]{1,0:T(8,128)(2,1)S(1)} %slice.158), channel_id=1, source_target_pairs={{0,4},{4,0},{8,12},{12,8},{16,20},{20,16},{24,28},{28,24},{1,5},{5... | collective-permute-start | bytes 1769480 | tf_op jit(solution)/shard_map/ppermute | solution.py:29
  157.7 19.5 %collective-permute-start.21 = (bf16[384,1024]{1,0:T(8,128)(2,1)S(1)}, bf16[384,1024]{1,0:T(8,128)(2,1)S(1)}, u32[]{:S(2)}, u32[]{:S(2)}) collective-permute-start(bf16[384,1024]{1,0:T(8,128)(2,1)S(1)} %convolution_convert_fusion.4), channel_id=1, source_target_pairs={{0,4},{4,0},{8,12},{12,8},{16,20},{20,16},{24,28},{28,24},{1,5},{5... | collective-permute-start | bytes 2359304 | tf_op jit(solution)/shard_map/ppermute | solution.py:29
  159.5 19.3 %collective-permute-start.20 = (bf16[768,512]{1,0:T(8,128)(2,1)S(1)}, bf16[768,512]{1,0:T(8,128)(2,1)S(1)}, u32[]{:S(2)}, u32[]{:S(2)}) collective-permute-start(bf16[768,512]{1,0:T(8,128)(2,1)S(1)} %convolution_convert_fusion.1), channel_id=1, source_target_pairs={{0,2},{1,3},{2,0},{3,1},{4,6},{5,7},{6,4},{7,5},{8,10},{9,11},{10,... | collective-permute-start | bytes 2359304 | tf_op jit(solution)/shard_map/ppermute | solution.py:29
  180.7 22.4 %collective-permute-start.22 = (bf16[384,512]{1,0:T(8,128)(2,1)S(1)}, bf16[384,512]{1,0:T(8,128)(2,1)S(1)}, u32[]{:S(2)}, u32[]{:S(2)}) collective-permute-start(bf16[384,512]{1,0:T(8,128)(2,1)S(1)} %slice.302), channel_id=1, source_target_pairs={{0,4},{4,0},{8,12},{12,8},{16,20},{20,16},{24,28},{28,24},{1,5},{5... | collective-permute-start | bytes 1179656 | tf_op jit(solution)/shard_map/ppermute | solution.py:29
  182.4 20.8 %collective-permute-start.23 = (bf16[384,512]{1,0:T(8,128)(2,1)S(1)}, bf16[384,512]{1,0:T(8,128)(2,1)S(1)}, u32[]{:S(2)}, u32[]{:S(2)}) collective-permute-start(bf16[384,512]{1,0:T(8,128)(2,1)S(1)} %slice.301), channel_id=1, source_target_pairs={{0,2},{1,3},{2,0},{3,1},{4,6},{5,7},{6,4},{7,5},{8,10},{9,11},{10,... | collective-permute-start | bytes 1179656 | tf_op jit(solution)/shard_map/ppermute | solution.py:29
  195.0 45.4 %collective-permute-start.25 = (bf16[768,384]{0,1:T(8,128)(2,1)S(1)}, bf16[768,384]{0,1:T(8,128)(2,1)S(1)}, u32[]{:S(2)}, u32[]{:S(2)}) collective-permute-start(bf16[768,384]{0,1:T(8,128)(2,1)S(1)} %pad_maximum_fusion.5), channel_id=1, source_target_pairs={{0,2},{1,3},{2,0},{3,1},{4,6},{5,7},{6,4},{7,5},{8,10},{9,11},{10,... | collective-permute-start | bytes 1769480 | tf_op jit(solution)/shard_map/ppermute | solution.py:29
  196.5 31.6 %collective-permute-start.24 = (bf16[768,512]{1,0:T(8,128)(2,1)S(1)}, bf16[768,512]{1,0:T(8,128)(2,1)S(1)}, u32[]{:S(2)}, u32[]{:S(2)}) collective-permute-start(bf16[768,512]{1,0:T(8,128)(2,1)S(1)} %convolution_convert_fusion.2), channel_id=1, source_target_pairs={{0,2},{1,3},{2,0},{3,1},{4,6},{5,7},{6,4},{7,5},{8,10},{9,11},{10,... | collective-permute-start | bytes 2359304 | tf_op jit(solution)/shard_map/ppermute | solution.py:29
  201.6 44.4 %collective-permute-start.34 = (bf16[384,384]{0,1:T(8,128)(2,1)S(1)}, bf16[384,384]{0,1:T(8,128)(2,1)S(1)}, u32[]{:S(2)}, u32[]{:S(2)}) collective-permute-start(bf16[384,384]{0,1:T(8,128)(2,1)S(1)} %fusion.20), channel_id=1, source_target_pairs={{0,2},{1,3},{2,0},{3,1},{4,6},{5,7},{6,4},{7,5},{8,10},{9,11},{10,... | collective-permute-start | bytes 884744 | tf_op jit(solution)/shard_map/ppermute | solution.py:29
  243.2 14.5 %collective-permute-start.30 = (bf16[384,512]{1,0:T(8,128)(2,1)S(1)}, bf16[384,512]{1,0:T(8,128)(2,1)S(1)}, u32[]{:S(2)}, u32[]{:S(2)}) collective-permute-start(bf16[384,512]{1,0:T(8,128)(2,1)S(1)} %slice.300), channel_id=1, source_target_pairs={{0,4},{4,0},{8,12},{12,8},{16,20},{20,16},{24,28},{28,24},{1,5},{5... | collective-permute-start | bytes 1179656 | tf_op jit(solution)/shard_map/ppermute | solution.py:29
  244.5 14.9 %collective-permute-start.28 = (bf16[192,1024]{1,0:T(8,128)(2,1)S(1)}, bf16[192,1024]{1,0:T(8,128)(2,1)S(1)}, u32[]{:S(2)}, u32[]{:S(2)}) collective-permute-start(bf16[192,1024]{1,0:T(8,128)(2,1)S(1)} %slice.299), channel_id=1, source_target_pairs={{0,8},{4,12},{8,0},{12,4},{16,24},{20,28},{24,16},{28,20},{1,9},{5... | collective-permute-start | bytes 1179656 | tf_op jit(solution)/shard_map/ppermute | solution.py:29
  267.0 15.3 %collective-permute-start.37 = (bf16[96,768]{0,1:T(8,128)(2,1)}, bf16[96,768]{0,1:T(8,128)(2,1)}, u32[]{:S(2)}, u32[]{:S(2)}) collective-permute-start(bf16[96,768]{0,1:T(8,128)(2,1)} %slice.304), channel_id=1, source_target_pairs={{0,16},{4,20},{8,24},{12,28},{16,0},{20,4},{24,8},{28,12},{1,17},{... | collective-permute-start | bytes 442376 | tf_op jit(solution)/shard_map/ppermute | solution.py:29
  296.5 20.9 %collective-permute-start.27 = (bf16[512,768]{1,0:T(8,128)(2,1)}, bf16[512,768]{1,0:T(8,128)(2,1)}, u32[]{:S(2)}, u32[]{:S(2)}) collective-permute-start(bf16[512,768]{1,0:T(8,128)(2,1)} %constant_dynamic-slice_fusion), channel_id=1, source_target_pairs={{0,1},{1,0},{2,3},{3,2},{4,5},{5,4},{6,7},{7,6},{8,9},{9,8},{10,11... | collective-permute-start | bytes 2359304 | tf_op jit(solution)/shard_map/ppermute | solution.py:29
  (109 other events, 975.9 us)
